TPU v7x, 32 devices: a whole 2x2x4 slice. The times are simulated.
32 devices in a mesh: groups: 2 (over y), blk: 4 (over z), head: 2 (over x), pair: 2 (over core).
Axes of the slice: x: 2, y: 2, z: 4, core: 2. Of those that a mesh axis runs over, the one named last changes fastest.
Arguments:
- single: bfloat16 [256, 384], P(('groups', 'blk')), parts along dimension 0, may hold values from -6 to 6
- pair: bfloat16 [256, 4, 32, 128], P(('groups', 'blk'), None, 'pair'), parts along dimension 0, may hold values from -6 to 6
- frames: float32 [12, 256], P(None, ('groups', 'blk')), parts along dimension 1, as said below
- chain: int32 [256], P(('groups', 'blk')), parts along dimension 0, may hold values from 0 to 5, never falling along the last dimension, each value on 1 to 42 neighbouring positions
- mask: int32 [256], P(('groups', 'blk')), parts along dimension 0, may hold values 0 or 1
- w_query: bfloat16 [384, 192], P(None, 'head'), may hold values from -0.3125 to 0.3125
- w_key_value: bfloat16 [384, 384], P(None, 'head'), may hold values from -0.3125 to 0.3125
- w_query_points: bfloat16 [384, 144], P(None, 'head'), may hold values from -0.3125 to 0.3125
- w_kv_points: bfloat16 [384, 432], P(None, 'head'), may hold values from -0.3125 to 0.3125
- w_pair_bias: bfloat16 [128, 12], P(None, 'head'), may hold values from -0.5 to 0.5
- head_weights: float32 [12], P('head'), may hold values from -9 to 1
- chain_bias: float32 [12], P('head'), may hold values from -3 to 3
- w_out: bfloat16 [12, 176, 384], P('head'), may hold values from -0.125 to 0.125
- out_gain: float32 [384], replicated, may hold values from 0.5 to 1.5
- w_backbone: bfloat16 [384, 6], replicated, may hold values from -0.3125 to 0.3125
Outputs:
- single_out: bfloat16 [256, 384], P(('groups', 'blk')), parts along dimension 0
- frames_out: float32 [12, 256], P(None, 'groups'), parts along dimension 1
There are 2 independent parts, one for each index of `groups`. A program takes and returns all parts, laid end to end along the dimension named above; an argument that names none is the same for every part. Nothing has to cross between parts.
Inputs may be any that keep to these rules, and one draw needn't show every extreme that they name: `frames`: rows 0 to 8 of every column hold an orthonormal rotation matrix row by row; rows 9 to 11 the translation.
All inputs are finite; a program needn't handle non-finite values. No bound on the sum of `mask` on one device may be relied on, other than what follows from the above.
Results may differ from a plain program's by a relative error of at most 0.0048.
Values sent between devices are 32-bit elements; how exact they have to be, the bound alone decides.
A program may use at most 64 MiB of HBM per device.

v0:
```python
import math

import jax
import jax.numpy as jnp
from jax import lax
from jax.sharding import PartitionSpec as P

HIGH = lax.Precision.HIGHEST
LOGIT_WEIGHT = math.sqrt(1.0 / 3.0)
MASK_PENALTY = 100000.0


def shifted(array, axis, by):
    peers = lax.axis_size(axis)
    return lax.ppermute(array, axis, [(i, (i + by) % peers) for i in range(peers)])


def combined_all(value, axis, join):
    pieces = jax.tree.map(lambda part: lax.all_gather(part, axis), value)
    head = jax.tree.map(lambda part: part[0], pieces)
    tail = jax.tree.map(lambda part: part[1:], pieces)
    so_far, _ = lax.scan(lambda so_far, section: (join(so_far, section), None), head, tail)
    return so_far


def to_global(local, frames):
    rotation = frames[:9].reshape(3, 3, -1)
    moved = jnp.einsum("abn,ngb->nga", rotation, local, precision=HIGH)
    return moved + jnp.transpose(frames[9:12])[:, None, :]


def to_local(points, frames):
    rotation = frames[:9].reshape(3, 3, -1)
    moved = points - jnp.transpose(frames[9:12])[:, None, None, :]
    return jnp.einsum("abn,nhpa->nhpb", rotation, moved, precision=HIGH)


def compose(frames, motion):
    rotation = frames[:9].reshape(3, 3, -1)
    inverse = 1.0 / jnp.sqrt(1.0 + motion[:, 0] ** 2 + motion[:, 1] ** 2 + motion[:, 2] ** 2)
    quat_b = motion[:, 0] * inverse
    quat_c = motion[:, 1] * inverse
    quat_d = motion[:, 2] * inverse
    spin = jnp.stack(
        [
            inverse * inverse + quat_b * quat_b - quat_c * quat_c - quat_d * quat_d,
            2.0 * (quat_b * quat_c - inverse * quat_d),
            2.0 * (quat_b * quat_d + inverse * quat_c),
            2.0 * (quat_b * quat_c + inverse * quat_d),
            inverse * inverse - quat_b * quat_b + quat_c * quat_c - quat_d * quat_d,
            2.0 * (quat_c * quat_d - inverse * quat_b),
            2.0 * (quat_b * quat_d - inverse * quat_c),
            2.0 * (quat_c * quat_d + inverse * quat_b),
            inverse * inverse - quat_b * quat_b - quat_c * quat_c + quat_d * quat_d,
        ]
    ).reshape(3, 3, -1)
    new_rotation = jnp.einsum("abn,bcn->acn", rotation, spin, precision=HIGH)
    offset = jnp.einsum("abn,nb->an", rotation, motion[:, 3:6], precision=HIGH)
    return jnp.concatenate([new_rotation.reshape(9, -1), frames[9:12] + offset], axis=0)


def attention_logits(
    pair_rows,
    query_rows,
    query_points,
    query_chain,
    query_present,
    keys,
    key_points,
    key_chain,
    key_present,
    w_pair_bias,
    distance_scale,
    chain_bias,
):
    count_q = pair_rows.shape[0]
    count_k = pair_rows.shape[1]
    bias = jnp.dot(
        pair_rows.reshape(count_q * count_k, -1), w_pair_bias, preferred_element_type=jnp.float32
    ).reshape(count_q, count_k, -1)
    dots = jnp.einsum("ihc,jhc->ijh", query_rows, keys, precision=HIGH) / math.sqrt(keys.shape[-1])
    gaps = query_points[:, None] - key_points[None]
    distance = jnp.sum(gaps * gaps, axis=(3, 4))
    differ = (query_chain[:, None] != key_chain[None, :]).astype(jnp.float32)
    logits = LOGIT_WEIGHT * (
        dots + bias - distance_scale * distance + chain_bias * differ[..., None]
    )
    absent = 1.0 - query_present[:, None] * key_present[None, :]
    return logits - MASK_PENALTY * absent[..., None]


def rescale(values, factor):
    return values * factor.reshape(factor.shape + (1,) * (values.ndim - factor.ndim))


def fold_pair(first, second):
    best = jnp.maximum(first[0], second[0])
    first_scale = jnp.exp(first[0] - best)
    second_scale = jnp.exp(second[0] - best)
    merged = [
        rescale(left_part, first_scale) + rescale(right_part, second_scale)
        for left_part, right_part in zip(first[1:], second[1:])
    ]
    return (best,) + tuple(merged)


def body(
    single,
    pair,
    frames,
    chain,
    mask,
    w_query,
    w_key_value,
    w_query_points,
    w_kv_points,
    w_pair_bias,
    head_weights,
    chain_bias,
    w_out,
    out_gain,
    w_backbone,
):
    rows = single.shape[0]
    half = pair.shape[2]
    width = pair.shape[3]
    heads_here = w_pair_bias.shape[1]
    head_size = w_query.shape[1] // heads_here
    query_count = w_query_points.shape[1] // (3 * heads_here)
    value_count = w_kv_points.shape[1] // (3 * heads_here) - query_count
    pair_keys = pair.reshape(rows, pair.shape[1] * half, width)
    query = jnp.dot(single, w_query, preferred_element_type=jnp.float32).reshape(
        rows, heads_here, head_size
    )
    query_local = jnp.dot(single, w_query_points, preferred_element_type=jnp.float32)
    query_points = to_global(query_local.reshape(rows, heads_here * query_count, 3), frames)
    query_points = query_points.reshape(rows, heads_here, query_count, 3)
    query_chain = chain.astype(jnp.float32)
    query_present = mask.astype(jnp.float32)
    distance_scale = jax.nn.softplus(head_weights) * math.sqrt(2.0 / (9.0 * query_count)) / 2.0
    position = lax.axis_index("pair")
    key_single = lax.dynamic_slice_in_dim(single, position * half, half, 0)
    key_frames = lax.dynamic_slice_in_dim(frames, position * half, half, 1)
    key_chain = lax.dynamic_slice_in_dim(query_chain, position * half, half, 0)
    key_present = lax.dynamic_slice_in_dim(query_present, position * half, half, 0)
    key_value = jnp.dot(key_single, w_key_value, preferred_element_type=jnp.float32)
    key_local = jnp.dot(key_single, w_kv_points, preferred_element_type=jnp.float32)
    key_global = to_global(
        key_local.reshape(half, heads_here * (query_count + value_count), 3), key_frames
    )
    payload = jnp.concatenate([key_value, key_global.reshape(half, -1)], axis=1)
    key_meta = jnp.stack([key_chain, key_present], axis=1)
    split_at = heads_here * 2 * head_size

    def absorb(carry, moving, moving_meta, start):
        top, total, sum_values, sum_points, sum_pair = carry
        count = moving.shape[0]
        pieces = moving[:, :split_at].reshape(count, heads_here, 2, head_size)
        points = moving[:, split_at:].reshape(count, heads_here, query_count + value_count, 3)
        pair_rows = lax.dynamic_slice_in_dim(pair_keys, start, count, 1)
        logits = attention_logits(
            pair_rows,
            query,
            query_points,
            query_chain,
            query_present,
            pieces[:, :, 0],
            points[:, :, :query_count],
            moving_meta[:, 0],
            moving_meta[:, 1],
            w_pair_bias,
            distance_scale,
            chain_bias,
        )
        new_top = jnp.maximum(top, jnp.max(logits, axis=1))
        scale = jnp.exp(top - new_top)
        weights = jnp.exp(logits - new_top[:, None, :])
        total = total * scale + jnp.sum(weights, axis=1)
        sum_values = sum_values * scale[..., None] + jnp.einsum(
            "ijh,jhc->ihc", weights, pieces[:, :, 1], precision=HIGH
        )
        sum_points = sum_points * scale[..., None, None] + jnp.einsum(
            "ijh,jhpd->ihpd", weights, points[:, :, query_count:], precision=HIGH
        )
        sum_pair = sum_pair * scale[..., None] + jnp.einsum(
            "ijh,ijc->ihc",
            weights.astype(jnp.bfloat16),
            pair_rows,
            preferred_element_type=jnp.float32,
        )
        return (new_top, total, sum_values, sum_points, sum_pair)

    initial = (
        jnp.full((rows, heads_here), -1e30, jnp.float32),
        jnp.zeros((rows, heads_here), jnp.float32),
        jnp.zeros((rows, heads_here, head_size), jnp.float32),
        jnp.zeros((rows, heads_here, value_count, 3), jnp.float32),
        jnp.zeros((rows, heads_here, width), jnp.float32),
    )
    block = lax.axis_index("blk")
    blocks = lax.axis_size("blk")
    carry = absorb(initial, payload, key_meta, block * half)

    def advance(step, state):
        carry, moving, moving_meta = state
        moving, moving_meta = shifted((moving, moving_meta), "blk", 1)
        source = (block - step) % blocks
        return (absorb(carry, moving, moving_meta, source * half), moving, moving_meta)

    carry = lax.fori_loop(1, blocks, advance, (carry, payload, key_meta))[0]
    best, total, sum_values, sum_points, sum_pair = combined_all(carry, "pair", fold_pair)
    attended = sum_values / total[..., None]
    pointed = to_local(sum_points / total[..., None, None], frames)
    point_norms = jnp.sqrt(jnp.sum(pointed * pointed, axis=3) + 1.0)
    paired = sum_pair / total[..., None]
    joined = jnp.concatenate(
        [attended, pointed.reshape(rows, heads_here, value_count * 3), point_norms, paired], axis=2
    ).astype(jnp.bfloat16)
    partial_update = jnp.dot(
        joined.reshape(rows, -1),
        w_out.reshape(-1, w_out.shape[2]),
        preferred_element_type=jnp.float32,
    )
    update = lax.psum(partial_update, "head")
    mixed = single.astype(jnp.float32) + update
    centre = jnp.mean(mixed, axis=1, keepdims=True)
    spread = jnp.mean(jnp.square(mixed - centre), axis=1, keepdims=True)
    single_out = ((mixed - centre) * lax.rsqrt(spread + 1e-05) * out_gain).astype(jnp.bfloat16)
    motion = jnp.dot(single_out, w_backbone, preferred_element_type=jnp.float32)
    frames_new = compose(frames, motion)
    frames_out = lax.all_gather(frames_new, "blk", axis=1, tiled=True)
    return (single_out, frames_out)


def solution(mesh):
    placed = (
        P(("groups", "blk"), None),
        P(("groups", "blk"), None, "pair", None),
        P(None, ("groups", "blk")),
        P(("groups", "blk")),
        P(("groups", "blk")),
        P(None, "head"),
        P(None, "head"),
        P(None, "head"),
        P(None, "head"),
        P(None, "head"),
        P("head"),
        P("head"),
        P("head", None, None),
        P(),
        P(),
    )
    return jax.shard_map(
        body,
        mesh=mesh,
        in_specs=placed,
        out_specs=(P(("groups", "blk"), None), P(None, "groups")),
        check_vma=False,
    )
```

profile of v0, /device:TPU:0, one launch (start us, length us, event | category | flops | bytes accessed | tf_op | source)
XLA Modules:
  0.0 85.5 jit_solution(7720689807309747148)
XLA Ops:
  0.7 0.7 copy-done.13
  3.1 1.1 %fusion.59 = f32[16,192]{1,0:T(8,128)S(1)} fusion(bf16[384,192]{0,1:T(8,128)(2,1)} %param.23, bf16[32,384]{1,0:T(8,128)(2,1)S(1)} %copy-done.3, s32[]{:T(128)S(6)} %select_n.43), kind=kOutput, calls=%fused_computation.96 | convolution fusion | flops 2359296 | bytes 172036 | tf_op jit(solution)/shard_map/dot_general | solution.py:146
  4.6 0.8 copy-done.7
  6.6 0.7 copy-done.4
  12.0 35.5 %while.7 = (s32[]{:T(128)}, f32[32,6]{0,1:T(8,128)S(1)}, f32[32,6]{0,1:T(8,128)S(1)}, f32[32,6,16]{0,2,1:T(8,128)S(1)}, f32[32,6,8,3]{0,2,3,1:T(8,128)S(1)}, /*i...) while((s32[]{:T(128)}, f32[32,6]{0,1:T(8,128)S(1)}, ...), condition=%wide.region_7.8_spmd, body=%wide.region_3.7_spmd.sunk | while | flops 3855250 | bytes 1648512 | solution.py:210
  12.0 3.1 %collective-permute-start = (f32[16,2]{0,1:T(2,128)S(1)}, f32[16,2]{0,1:T(2,128)S(1)}, u32[]{:S(2)}, u32[]{:S(2)}) collective-permute-start(f32[16,2]{0,1:T(2,128)S(1)} %get-tuple-element.757), channel_id=1, source_target_pairs={{0,4},{4,8},{8,12},{12,0},{1,5},{5,9},{9,13},{13,1},{2,6},{6,10},{... | collective-permute-start | bytes 392 | tf_op jit(solution)/shard_map/while/body/eval_jaxpr/ppermute | solution.py:15
  15.1 1.6 %collective-permute-start.1 = (f32[16,408]{0,1:T(8,128)S(1)}, f32[16,408]{0,1:T(8,128)S(1)}, u32[]{:S(2)}, u32[]{:S(2)}) collective-permute-start(f32[16,408]{0,1:T(8,128)S(1)} %get-tuple-element.756), channel_id=1, source_target_pairs={{0,4},{4,8},{8,12},{12,0},{1,5},{5,9},{9,13},{13,1},{2,6},{6,10},{... | collective-permute-start | bytes 78344 | tf_op jit(solution)/shard_map/while/body/eval_jaxpr/ppermute | solution.py:15
  17.2 1.5 %collective-permute-done = f32[16,2]{0,1:T(2,128)S(1)} collective-permute-done((f32[16,2]{0,1:T(2,128)S(1)}, f32[16,2]{0,1:T(2,128)S(1)}, u32[]{:S(2)}, u32[]{:S(2)}) %collective-permute-start) | collective-permute-done | bytes 160 | tf_op jit(solution)/shard_map/while/body/eval_jaxpr/ppermute | solution.py:15
  18.9 4.7 %collective-permute-done.1 = f32[16,408]{0,1:T(8,128)S(1)} collective-permute-done((f32[16,408]{0,1:T(8,128)S(1)}, f32[16,408]{0,1:T(8,128)S(1)}, u32[]{:S(2)}, u32[]{:S(2)}) %collective-permute-start.1) | collective-permute-done | bytes 26144 | tf_op jit(solution)/shard_map/while/body/eval_jaxpr/ppermute | solution.py:15
  23.7 0.6 copy-done.1
  26.5 1.4 %collective-permute-start.1 = (f32[16,408]{0,1:T(8,128)S(1)}, f32[16,408]{0,1:T(8,128)S(1)}, u32[]{:S(2)}, u32[]{:S(2)}) collective-permute-start(f32[16,408]{0,1:T(8,128)S(1)} %get-tuple-element.756), channel_id=1, source_target_pairs={{0,4},{4,8},{8,12},{12,0},{1,5},{5,9},{9,13},{13,1},{2,6},{6,10},{... | collective-permute-start | bytes 78344 | tf_op jit(solution)/shard_map/while/body/eval_jaxpr/ppermute | solution.py:15
  28.3 3.5 %collective-permute-done = f32[16,2]{0,1:T(2,128)S(1)} collective-permute-done((f32[16,2]{0,1:T(2,128)S(1)}, f32[16,2]{0,1:T(2,128)S(1)}, u32[]{:S(2)}, u32[]{:S(2)}) %collective-permute-start) | collective-permute-done | bytes 160 | tf_op jit(solution)/shard_map/while/body/eval_jaxpr/ppermute | solution.py:15
  32.0 2.1 %collective-permute-done.1 = f32[16,408]{0,1:T(8,128)S(1)} collective-permute-done((f32[16,408]{0,1:T(8,128)S(1)}, f32[16,408]{0,1:T(8,128)S(1)}, u32[]{:S(2)}, u32[]{:S(2)}) %collective-permute-start.1) | collective-permute-done | bytes 26144 | tf_op jit(solution)/shard_map/while/body/eval_jaxpr/ppermute | solution.py:15
  38.2 4.3 %collective-permute-done = f32[16,2]{0,1:T(2,128)S(1)} collective-permute-done((f32[16,2]{0,1:T(2,128)S(1)}, f32[16,2]{0,1:T(2,128)S(1)}, u32[]{:S(2)}, u32[]{:S(2)}) %collective-permute-start) | collective-permute-done | bytes 160 | tf_op jit(solution)/shard_map/while/body/eval_jaxpr/ppermute | solution.py:15
  42.6 2.1 %collective-permute-done.1 = f32[16,408]{0,1:T(8,128)S(1)} collective-permute-done((f32[16,408]{0,1:T(8,128)S(1)}, f32[16,408]{0,1:T(8,128)S(1)}, u32[]{:S(2)}, u32[]{:S(2)}) %collective-permute-start.1) | collective-permute-done | bytes 26144 | tf_op jit(solution)/shard_map/while/body/eval_jaxpr/ppermute | solution.py:15
  47.6 1.8 %all-gather.5 = f32[2,32,6]{1,2,0:T(8,128)S(1)} all-gather(f32[1,32,6]{1,2,0:T(8,128)S(1)} %bitcast.281), channel_id=3, replica_groups=mesh['groups'=2,'blk'=4,'head'=2,'pair'=2] {'pair'}, dimensions={0}, use_global_device_ids=true | all-gather | bytes 2304 | tf_op jit(solution)/shard_map/all_gather | solution.py:19
  49.4 1.8 %all-gather.6 = f32[2,32,6]{1,2,0:T(8,128)S(1)} all-gather(f32[1,32,6]{1,2,0:T(8,128)S(1)} %bitcast.282), channel_id=4, replica_groups=mesh['groups'=2,'blk'=4,'head'=2,'pair'=2] {'pair'}, dimensions={0}, use_global_device_ids=true | all-gather | bytes 2304 | tf_op jit(solution)/shard_map/all_gather | solution.py:19
  51.5 1.9 %all-gather.4 = f32[64,6,128]{2,0,1:T(8,128)S(1)} all-gather(f32[32,6,128]{2,0,1:T(8,128)S(1)} %copy.259), channel_id=6, replica_groups=mesh['groups'=2,'blk'=4,'head'=2,'pair'=2] {'pair'}, dimensions={0}, use_global_device_ids=true | all-gather | bytes 294912 | tf_op jit(solution)/shard_map/all_gather | solution.py:19
  53.7 1.9 %all-gather = f32[64,6,16]{2,0,1:T(8,128)S(1)} all-gather(f32[32,6,16]{2,0,1:T(8,128)S(1)} %copy.249), channel_id=2, replica_groups=mesh['groups'=2,'blk'=4,'head'=2,'pair'=2] {'pair'}, dimensions={0}, use_global_device_ids=true | all-gather | bytes 36864 | tf_op jit(solution)/shard_map/all_gather | solution.py:19
  56.0 2.4 %all-gather.3 = f32[64,6,8,3]{2,1,3,0:T(8,128)S(1)} all-gather(f32[32,6,8,3]{2,1,3,0:T(8,128)S(1)} %copy.250), channel_id=5, replica_groups=mesh['groups'=2,'blk'=4,'head'=2,'pair'=2] {'pair'}, dimensions={0}, use_global_device_ids=true | all-gather | bytes 55296 | tf_op jit(solution)/shard_map/all_gather | solution.py:19
  58.6 1.1 %fusion.82 = (bf16[32,6,8,3]{2,3,1,0:T(4,128)(2,1)S(1)}, f32[32,6,8]{2,1,0:T(8,128)S(1)}) fusion(f32[3,3,32,1]{0,1,3,2:T(4,128)S(1)} %copy.271, f32[32,6,8,3]{2,1,3,0:T(8,128)S(1)} %fusion.30), kind=kOutput, calls=%fused_computation.152 | convolution fusion | flops 178176 | bytes 34944 | tf_op jit(solution)/shard_map/abn,nhpa->nhpb/dot_general | solution.py:35
  60.7 8.6 %psum.7 = f32[32,384]{1,0:T(8,128)S(1)} all-reduce(f32[32,384]{1,0:T(8,128)S(1)} %convolution_bitcast_fusion.4), channel_id=1, replica_groups=mesh['groups'=2,'blk'=4,'head'=2,'pair'=2] {'head'}, use_global_device_ids=true, to_apply=%region_9.10 | all-reduce | flops 12288 | bytes 98304 | tf_op jit(solution)/shard_map/psum | solution.py:224
  71.6 13.1 %all-gather.7 = f32[4,32,12]{1,2,0:T(8,128)S(1)} all-gather(f32[1,32,12]{1,2,0:T(8,128)S(1)} %maximum_bitcast_fusion), channel_id=1, replica_groups=mesh['groups'=2,'blk'=4,'head'=2,'pair'=2] {'blk'}, dimensions={0}, use_global_device_ids=true | all-gather | bytes 7680 | tf_op jit(solution)/shard_map/all_gather | solution.py:231
  84.8 0.7 reshape.714
  (200 shorter events, 22.4 us)
Async XLA Ops:
  0.6 59.6 %copy-start = (bf16[6,176,384]{2,1,0:T(8,128)(2,1)S(1)}, bf16[6,176,384]{2,1,0:T(8,128)(2,1)}, u32[]{:S(2)}) copy-start(bf16[6,176,384]{2,1,0:T(8,128)(2,1)} %param.29) | copy-start | bytes 2433028
  0.7 0.7 copy-start.13
  0.7 0.7 copy-start.14
  0.7 0.7 copy-start.15
  1.4 0.7 copy-start.8
  2.4 0.7 copy-start.3
  3.1 1.2 %copy-start.9 = (bf16[384,72]{0,1:T(8,128)(2,1)S(1)}, bf16[384,72]{0,1:T(8,128)(2,1)}, u32[]{:S(2)}) copy-start(bf16[384,72]{0,1:T(8,128)(2,1)} %param.24) | copy-start | bytes 165892
  4.5 0.9 %copy-start.7 = (bf16[384,96]{0,1:T(8,128)(2,1)S(1)}, bf16[384,96]{0,1:T(8,128)(2,1)}, u32[]{:S(2)}) copy-start(bf16[384,96]{0,1:T(8,128)(2,1)} %param.22) | copy-start | bytes 221188
  6.5 0.9 %copy-start.4 = (bf16[384,216]{0,1:T(8,128)(2,1)S(1)}, bf16[384,216]{0,1:T(8,128)(2,1)}, u32[]{:S(2)}) copy-start(bf16[384,216]{0,1:T(8,128)(2,1)} %param.25) | copy-start | bytes 497668
  7.6 1.0 %copy-start.2 = (bf16[32,4,16,128]{3,2,1,0:T(8,128)(2,1)S(1)}, bf16[32,4,16,128]{3,2,1,0:T(8,128)(2,1)}, u32[]{:S(2)}) copy-start(bf16[32,4,16,128]{3,2,1,0:T(8,128)(2,1)} %param.18) | copy-start | bytes 1572868
  8.3 0.7 copy-start.6
  9.8 0.7 copy-start.10
  12.0 6.7 %collective-permute-start = (f32[16,2]{0,1:T(2,128)S(1)}, f32[16,2]{0,1:T(2,128)S(1)}, u32[]{:S(2)}, u32[]{:S(2)}) collective-permute-start(f32[16,2]{0,1:T(2,128)S(1)} %get-tuple-element.757), channel_id=1, source_target_pairs={{0,4},{4,8},{8,12},{12,0},{1,5},{5,9},{9,13},{13,1},{2,6},{6,10},{... | collective-permute-start | bytes 392 | tf_op jit(solution)/shard_map/while/body/eval_jaxpr/ppermute | solution.py:15
  15.1 8.4 %collective-permute-start.1 = (f32[16,408]{0,1:T(8,128)S(1)}, f32[16,408]{0,1:T(8,128)S(1)}, u32[]{:S(2)}, u32[]{:S(2)}) collective-permute-start(f32[16,408]{0,1:T(8,128)S(1)} %get-tuple-element.756), channel_id=1, source_target_pairs={{0,4},{4,8},{8,12},{12,0},{1,5},{5,9},{9,13},{13,1},{2,6},{6,10},{... | collective-permute-start | bytes 78344 | tf_op jit(solution)/shard_map/while/body/eval_jaxpr/ppermute | solution.py:15
  23.6 0.7 copy-start.1
  25.0 0.9 %slice-start = ((f32[16,6,12,3]{0,3,2,1:T(4,128)}), f32[16,6,8,3]{0,3,2,1:T(4,128)S(1)}, s32[]{:S(2)}) async-start(f32[16,6,12,3]{0,3,2,1:T(4,128)} %copy-done.1), calls=%async_computation | async-start | bytes 196608 | tf_op jit(solution)/shard_map/while/body/eval_jaxpr/slice | solution.py:183
  26.4 5.4 %collective-permute-start = (f32[16,2]{0,1:T(2,128)S(1)}, f32[16,2]{0,1:T(2,128)S(1)}, u32[]{:S(2)}, u32[]{:S(2)}) collective-permute-start(f32[16,2]{0,1:T(2,128)S(1)} %get-tuple-element.757), channel_id=1, source_target_pairs={{0,4},{4,8},{8,12},{12,0},{1,5},{5,9},{9,13},{13,1},{2,6},{6,10},{... | collective-permute-start | bytes 392 | tf_op jit(solution)/shard_map/while/body/eval_jaxpr/ppermute | solution.py:15
  26.5 7.7 %collective-permute-start.1 = (f32[16,408]{0,1:T(8,128)S(1)}, f32[16,408]{0,1:T(8,128)S(1)}, u32[]{:S(2)}, u32[]{:S(2)}) collective-permute-start(f32[16,408]{0,1:T(8,128)S(1)} %get-tuple-element.756), channel_id=1, source_target_pairs={{0,4},{4,8},{8,12},{12,0},{1,5},{5,9},{9,13},{13,1},{2,6},{6,10},{... | collective-permute-start | bytes 78344 | tf_op jit(solution)/shard_map/while/body/eval_jaxpr/ppermute | solution.py:15
  35.6 0.9 %slice-start = ((f32[16,6,12,3]{0,3,2,1:T(4,128)}), f32[16,6,8,3]{0,3,2,1:T(4,128)S(1)}, s32[]{:S(2)}) async-start(f32[16,6,12,3]{0,3,2,1:T(4,128)} %copy-done.1), calls=%async_computation | async-start | bytes 196608 | tf_op jit(solution)/shard_map/while/body/eval_jaxpr/slice | solution.py:183
  37.0 5.4 %collective-permute-start = (f32[16,2]{0,1:T(2,128)S(1)}, f32[16,2]{0,1:T(2,128)S(1)}, u32[]{:S(2)}, u32[]{:S(2)}) collective-permute-start(f32[16,2]{0,1:T(2,128)S(1)} %get-tuple-element.757), channel_id=1, source_target_pairs={{0,4},{4,8},{8,12},{12,0},{1,5},{5,9},{9,13},{13,1},{2,6},{6,10},{... | collective-permute-start | bytes 392 | tf_op jit(solution)/shard_map/while/body/eval_jaxpr/ppermute | solution.py:15
  37.1 7.7 %collective-permute-start.1 = (f32[16,408]{0,1:T(8,128)S(1)}, f32[16,408]{0,1:T(8,128)S(1)}, u32[]{:S(2)}, u32[]{:S(2)}) collective-permute-start(f32[16,408]{0,1:T(8,128)S(1)} %get-tuple-element.756), channel_id=1, source_target_pairs={{0,4},{4,8},{8,12},{12,0},{1,5},{5,9},{9,13},{13,1},{2,6},{6,10},{... | collective-permute-start | bytes 78344 | tf_op jit(solution)/shard_map/while/body/eval_jaxpr/ppermute | solution.py:15
  46.1 0.9 %slice-start = ((f32[16,6,12,3]{0,3,2,1:T(4,128)}), f32[16,6,8,3]{0,3,2,1:T(4,128)S(1)}, s32[]{:S(2)}) async-start(f32[16,6,12,3]{0,3,2,1:T(4,128)} %copy-done.1), calls=%async_computation | async-start | bytes 196608 | tf_op jit(solution)/shard_map/while/body/eval_jaxpr/slice | solution.py:183
  60.3 9.3 %copy-start.12 = (f32[384]{0:T(512)S(1)}, f32[384]{0:T(512)}, u32[]{:S(2)}) copy-start(f32[384]{0:T(512)} %param.30) | copy-start | bytes 4612
  69.6 0.7 copy-start.11
  (3 other events, 1.9 us)
where the time goes:
time: 86 us; the launch traced here: 85.5 us
  blocking collectives  31.6 us (37%)
  waiting for transfers between devices  18.2 us (21%)
  local copies, waits for them, and re-layouts  15 us (17%)
  matrix products  9.58 us (11%)
  starting transfers between devices  6.74 us (8%)
  other arithmetic  2.83 us (3%)
  between operations  1.1 us (1%)
    ppermute x6, waiting for transfers between devices, shifted(): lax.ppermute(array, axis, [(i, (i + by) % peers) for i in range(peers)])  18.2 us
    all_gather x1, blocking collectives, body(): frames_out = lax.all_gather(frames_new, 'blk', axis=1, tiled=True)  13.1 us
    all_gather x5, blocking collectives, combined_all(): pieces = jax.tree.map(lambda part: lax.all_gather(part, axis), value)  9.88 us
    psum x1, blocking collectives, body(): update = lax.psum(partial_update, 'head')  8.59 us
    ppermute x6, starting transfers between devices, shifted(): lax.ppermute(array, axis, [(i, (i + by) % peers) for i in range(peers)])  6.74 us
    unnamed x32, local copies, waits for them, and re-layouts  6.07 us
    while x15, local copies, waits for them, and re-layouts  1.94 us
    slice x7, local copies, waits for them, and re-layouts, absorb(): points[:, :, query_count:]  1.86 us
  transfers between devices with their start and end apart: 6, of which 6 were waited for; matrix products, arithmetic and copies ran while one was open for 2% of the time, Pallas kernels for 0%

commit v1 on v0

v1 whole, which is shorter than its diff:
```python
import functools
import math

import jax
import jax.numpy as jnp
import numpy as np
from jax import lax
from jax.experimental import pallas as pl
from jax.experimental.pallas import tpu as pltpu
from jax.sharding import PartitionSpec as P

LOGIT_WEIGHT = math.sqrt(1.0 / 3.0)
MASK_PENALTY = 100000.0
MESH = pl.DeviceIdType.MESH
LANES = 128
SUB = 8


def up(value, unit):
    return -(-value // unit) * unit


def nt(a, b):
    return lax.dot_general(a, b, (((1,), (1,)), ((), ())), preferred_element_type=jnp.float32)


def nn(a, b):
    return lax.dot_general(a, b, (((1,), (0,)), ((), ())), preferred_element_type=jnp.float32)


def halves(value):
    high = value.astype(jnp.bfloat16)
    return high, (value - high.astype(jnp.float32)).astype(jnp.bfloat16)


def dot3(product, a, b):
    a_high, a_low = halves(a)
    b_high, b_low = halves(b)
    return product(a_high, b_high) + (product(a_low, b_high) + product(a_high, b_low))


def selectors(heads, size, queries, values):
    wide = up(heads * max(size, values), LANES)
    sel_q = np.zeros((3 * queries * SUB, heads * queries * 3), np.float32)
    key_rows = up(heads * size, 16)
    sel_kv = np.zeros((key_rows + wide, heads * 2 * size), np.float32)
    sel_kp = np.zeros((3 * queries * SUB + 3 * wide, heads * (queries + values) * 3), np.float32)
    small = size + 4 * values
    sel_out = np.zeros((5 * wide, heads * small), np.float32)
    for h in range(heads):
        for b in range(3):
            for p in range(queries):
                row = (b * queries + p) * SUB + h
                sel_q[row, (h * queries + p) * 3 + b] = 1
                sel_kp[row, (h * (queries + values) + p) * 3 + b] = 1
            for p in range(values):
                row = 3 * queries * SUB + b * wide + h * values + p
                sel_kp[row, (h * (queries + values) + queries + p) * 3 + b] = 1
                sel_out[(1 + b) * wide + h * values + p, h * small + size + p * 3 + b] = 1
        for p in range(values):
            sel_out[4 * wide + h * values + p, h * small + size + 3 * values + p] = 1
        for c in range(size):
            sel_kv[h * size + c, h * 2 * size + c] = 1
            sel_kv[key_rows + h * size + c, h * 2 * size + size + c] = 1
            sel_out[h * size + c, h * small + c] = 1
    return [jnp.asarray(s, jnp.bfloat16) for s in (sel_q, sel_kv, sel_kp, sel_out)]


def kernel(
    dims,
    single_ref, pair_hbm, frames_ref, chain_row_ref, mask_row_ref, chain_ref, mask_ref,
    wq_ref, wkv_ref, wqp_ref, wkp_ref, wpb_ref, hw_ref, cb_ref, wout_hbm, gain_ref, wbb_ref,
    selq_ref, selkv_ref, selkp_ref, selout_ref,
    so_ref, fo_ref,
    gath, meta_s, pair_v, wout_v, sp, ex, red, fg,
    load_sem, gs_sem, gr_sem, es_sem, er_sem, rs_sem, rr_sem, fs_sem, fr_sem,
):
    nb, nh, npr, heads, size, queries, values = dims
    rows, width = single_ref.shape
    half = rows // npr
    keys = nb * half
    wide = up(heads * max(size, values), LANES)
    me_b = lax.axis_index("blk")
    me_h = lax.axis_index("head")
    me_p = lax.axis_index("pair")
    f32, bf16 = jnp.float32, jnp.bfloat16

    def blk_peer(d):
        return {"blk": lax.rem(me_b + d, nb)}

    def group_peer(dh, dp):
        return {"head": lax.rem(me_h + dh, nh), "pair": lax.rem(me_p + dp, npr)}

    group = [(dh, dp) for dh in range(nh) for dp in range(npr) if dh or dp]
    load_pair = pltpu.make_async_copy(pair_hbm, pair_v, load_sem.at[0])
    load_pair.start()
    load_out = pltpu.make_async_copy(wout_hbm, wout_v, load_sem.at[1])
    load_out.start()
    barrier = pltpu.get_barrier_semaphore()
    for d in range(1, nb):
        pl.semaphore_signal(barrier, inc=1, device_id=blk_peer(d), device_id_type=MESH)
    for dh, dp in group:
        pl.semaphore_signal(barrier, inc=1, device_id=group_peer(dh, dp), device_id_type=MESH)

    frames = frames_ref[...]
    meta = jnp.concatenate(
        [
            frames,
            chain_row_ref[...].astype(f32),
            mask_row_ref[...].astype(f32),
            jnp.zeros((LANES - 14, rows), f32),
        ],
        axis=0,
    ).T
    meta_s[...] = meta
    start = pl.multiple_of(me_p * half, half)
    gath[me_b, :, :width] = single_ref[pl.ds(start, half), :].astype(f32)
    gath[me_b, :, width:] = meta_s[pl.ds(start, half), :]

    single = single_ref[...]
    w_kv = nt(selkv_ref[...], wkv_ref[...]).astype(bf16)
    w_kp = nt(selkp_ref[...], wkp_ref[...]).astype(bf16)

    pl.semaphore_wait(barrier, nb - 1 + len(group))
    gathers = []
    for d in range(1, nb):
        copy = pltpu.make_async_remote_copy(
            src_ref=gath.at[me_b],
            dst_ref=gath.at[me_b],
            send_sem=gs_sem.at[d],
            recv_sem=gr_sem.at[d],
            device_id=blk_peer(d),
            device_id_type=MESH,
        )
        copy.start()
        gathers.append(copy)

    w_qp = nt(selq_ref[...], wqp_ref[...]).astype(bf16)
    query = nn(single, wq_ref[...]) * (1.0 / math.sqrt(size))
    q_local = nt(w_qp, single)
    step = queries * SUB

    def moved(local, base, count, turn):
        out = []
        for a in range(3):
            total = turn[9 + a : 10 + a]
            mixed = sum(
                turn[3 * a + b : 3 * a + b + 1] * local[base + b * count : base + (b + 1) * count]
                for b in range(3)
            )
            out.append(mixed + total)
        return out

    q_global = moved(q_local, 0, step, frames)
    eye = (
        lax.broadcasted_iota(jnp.int32, (SUB, heads), 0)
        == lax.broadcasted_iota(jnp.int32, (SUB, heads), 1)
    ).astype(bf16)
    w_bias = nt(eye, wpb_ref[...]).astype(bf16)
    eye6 = (
        lax.broadcasted_iota(jnp.int32, (SUB, wbb_ref.shape[1]), 0)
        == lax.broadcasted_iota(jnp.int32, (SUB, wbb_ref.shape[1]), 1)
    ).astype(bf16)
    w_back = nt(eye6, wbb_ref[...]).astype(bf16)
    head_row = lax.broadcasted_iota(jnp.int32, (SUB, keys), 0)
    raw = jnp.zeros((SUB, keys), f32)
    chain_term = jnp.zeros((SUB, keys), f32)
    for h in range(heads):
        raw = jnp.where(head_row == h, hw_ref[h], raw)
        chain_term = jnp.where(head_row == h, cb_ref[h], chain_term)
    soft = jnp.maximum(raw, 0.0) + jnp.log1p(jnp.exp(-jnp.abs(raw)))
    distance_scale = soft * (math.sqrt(2.0 / (9.0 * queries)) / 2.0)
    own_head = (
        lax.broadcasted_iota(jnp.int32, (SUB, heads * size), 1) // size
        == lax.broadcasted_iota(jnp.int32, (SUB, heads * size), 0)
    ).astype(f32)
    q_wide = (query[:, None, :] * own_head[None]).reshape(rows * SUB, heads * size)
    load_pair.wait()
    pairs = [pair_v[i * keys : (i + 1) * keys, :] for i in range(rows)]
    biases = [nt(w_bias, pairs[i]) for i in range(rows)]
    load_out.wait()
    small = size + 4 * values
    w_small = nn(
        selout_ref[...], jnp.concatenate([wout_v[h, :small, :] for h in range(heads)], axis=0)
    ).astype(bf16)

    for copy in gathers:
        copy.wait()
    everyone = gath[...].reshape(keys, width + LANES)
    key_single = everyone[:, :width].astype(bf16)
    key_meta = everyone[:, width:].T
    kv = nt(w_kv, key_single)
    key_rows = up(heads * size, 16)
    kp = nt(w_kp, key_single)
    k_global = moved(kp, 0, step, key_meta)
    v_global = moved(kp, 3 * step, wide, key_meta)
    dots = dot3(nn, q_wide, kv[: heads * size])
    key_chain = jnp.broadcast_to(key_meta[12:13], (SUB, keys))
    key_present = jnp.broadcast_to(key_meta[13:14], (SUB, keys))

    weights, tops, totals = [], [], []
    for i in range(rows):
        distance = jnp.zeros((SUB, keys), f32)
        for a in range(3):
            for p in range(queries):
                gap = (
                    q_global[a][p * SUB : (p + 1) * SUB, i : i + 1]
                    - k_global[a][p * SUB : (p + 1) * SUB, :]
                )
                distance = distance + gap * gap
        differ = jnp.where(key_chain != chain_ref[i].astype(f32), chain_term, 0.0)
        logits = LOGIT_WEIGHT * (
            dots[i * SUB : (i + 1) * SUB] + biases[i] - distance_scale * distance + differ
        )
        absent = 1.0 - mask_ref[i].astype(f32) * key_present
        logits = logits - MASK_PENALTY * absent
        top = jnp.max(logits, axis=1, keepdims=True)
        weight = jnp.exp(logits - top)
        weights.append(weight)
        tops.append(jnp.broadcast_to(top, (SUB, LANES)))
        totals.append(jnp.broadcast_to(jnp.sum(weight, axis=1, keepdims=True), (SUB, LANES)))

    lane = lax.broadcasted_iota(jnp.int32, (SUB, LANES), 1)
    row = lax.broadcasted_iota(jnp.int32, (SUB, LANES), 0)
    stat = jnp.concatenate(
        [
            jnp.sum(
                jnp.where(lane == row, tops[i], jnp.where(lane == row + SUB, totals[i], 0.0)),
                axis=0,
                keepdims=True,
            )
            for i in range(rows)
        ],
        axis=0,
    )
    wide_lane = lax.broadcasted_iota(jnp.int32, (SUB, wide), 1)
    wide_row = lax.broadcasted_iota(jnp.int32, (SUB, wide), 0)
    keep_value = (wide_lane // size == wide_row).astype(f32)
    keep_point = (wide_lane // values == wide_row).astype(f32)
    keep = jnp.concatenate([keep_value, keep_point, keep_point, keep_point], axis=1)
    every = jnp.concatenate(weights, axis=0)
    sums = dot3(nt, every, jnp.concatenate([kv[key_rows:]] + v_global, axis=0))
    sums = jnp.sum(sums.reshape(rows, SUB, 4 * wide) * keep[None], axis=1)
    ex[0, :, :LANES] = stat
    ex[0, :, LANES:] = sums[:, wide:]
    exchanges = []
    for d in range(1, npr):
        copy = pltpu.make_async_remote_copy(
            src_ref=ex.at[0],
            dst_ref=ex.at[d],
            send_sem=es_sem.at[d],
            recv_sem=er_sem.at[d],
            device_id=group_peer(0, d),
            device_id_type=MESH,
        )
        copy.start()
        exchanges.append(copy)

    for i in range(rows):
        sp[i * SUB : (i + 1) * SUB, :] = nn(weights[i].astype(bf16), pairs[i])

    for copy in exchanges:
        copy.wait()
    stats = [stat] + [ex[d, :, :LANES] for d in range(1, npr)]
    best = functools.reduce(jnp.maximum, [s[:, :SUB] for s in stats])
    scales = [jnp.exp(s[:, :SUB] - best) for s in stats]
    total = sum(s[:, SUB : 2 * SUB] * scale for s, scale in zip(stats, scales))
    factors = [scale / total for scale in scales]
    full_lane = lax.broadcasted_iota(jnp.int32, (rows, wide), 1)

    def spread(factor, count):
        out = jnp.zeros((rows, wide), f32)
        for h in range(heads):
            out = jnp.where(full_lane // count == h, factor[:, h : h + 1], out)
        return out

    attended = sums[:, :wide] * spread(factors[0], size)
    pointed_global = []
    for a in range(3):
        pointed_global.append(sums[:, (1 + a) * wide : (2 + a) * wide] * spread(factors[0], values))
    for d in range(1, npr):
        scale = spread(factors[d], values)
        for a in range(3):
            base = LANES + a * wide
            pointed_global[a] = pointed_global[a] + ex[d, :, base : base + wide] * scale
    shifted = [pointed_global[a] - meta[:, 9 + a : 10 + a] for a in range(3)]
    pointed = [
        sum(meta[:, 3 * a + b : 3 * a + b + 1] * shifted[a] for a in range(3)) for b in range(3)
    ]
    norms = jnp.sqrt(sum(p * p for p in pointed) + 1.0)
    features = [attended] + [p * (1.0 / npr) for p in pointed + [norms]]
    partial = sum(
        nn(feature.astype(bf16), w_small[k * wide : (k + 1) * wide])
        for k, feature in enumerate(features)
    )
    for h in range(heads):
        paired = sp[pl.ds(h, rows, stride=SUB), :] * factors[0][:, h : h + 1]
        partial = partial + nn(paired.astype(bf16), wout_v[h, small:, :])
    red[0] = partial
    reductions = []
    for dh, dp in group:
        code = dh * npr + dp
        copy = pltpu.make_async_remote_copy(
            src_ref=red.at[0],
            dst_ref=red.at[code],
            send_sem=rs_sem.at[code],
            recv_sem=rr_sem.at[code],
            device_id=group_peer(dh, dp),
            device_id_type=MESH,
        )
        copy.start()
        reductions.append(copy)
    for copy in reductions:
        copy.wait()
    update = jnp.zeros((rows, width), f32)
    for h in range(nh):
        for p in range(npr):
            code = lax.rem(me_h - h + nh, nh) * npr + lax.rem(me_p - p + npr, npr)
            update = update + red[code]
    mixed = single.astype(f32) + update
    centre = jnp.mean(mixed, axis=1, keepdims=True)
    away = mixed - centre
    variance = jnp.mean(away * away, axis=1, keepdims=True)
    out = (away * lax.rsqrt(variance + 1e-05) * gain_ref[...]).astype(bf16)
    so_ref[...] = out
    motion = nt(w_back, out)
    m = [motion[k : k + 1] for k in range(6)]
    inverse = 1.0 / jnp.sqrt(1.0 + m[0] * m[0] + m[1] * m[1] + m[2] * m[2])
    qa, qb, qc, qd = inverse, m[0] * inverse, m[1] * inverse, m[2] * inverse
    spin = [
        qa * qa + qb * qb - qc * qc - qd * qd,
        2.0 * (qb * qc - qa * qd),
        2.0 * (qb * qd + qa * qc),
        2.0 * (qb * qc + qa * qd),
        qa * qa - qb * qb + qc * qc - qd * qd,
        2.0 * (qc * qd - qa * qb),
        2.0 * (qb * qd - qa * qc),
        2.0 * (qc * qd + qa * qb),
        qa * qa - qb * qb - qc * qc + qd * qd,
    ]
    turn = [frames[k : k + 1] for k in range(12)]
    lines = [
        sum(turn[3 * a + b] * spin[3 * b + c] for b in range(3)) for a in range(3) for c in range(3)
    ]
    lines += [
        turn[9 + a] + sum(turn[3 * a + b] * m[3 + b] for b in range(3)) for a in range(3)
    ]
    fg[me_b] = jnp.concatenate(lines + [jnp.zeros((4, rows), f32)], axis=0)
    finals = []
    for d in range(1, nb):
        copy = pltpu.make_async_remote_copy(
            src_ref=fg.at[me_b],
            dst_ref=fg.at[me_b],
            send_sem=fs_sem.at[d],
            recv_sem=fr_sem.at[d],
            device_id=blk_peer(d),
            device_id_type=MESH,
        )
        copy.start()
        finals.append(copy)
    for copy in finals:
        copy.wait()
    for k in range(nb):
        fo_ref[:, k * rows : (k + 1) * rows] = fg[k, :12, :]


def body(
    single, pair, frames, chain, mask, w_query, w_key_value, w_query_points, w_kv_points,
    w_pair_bias, head_weights, chain_bias, w_out, out_gain, w_backbone,
):
    nb, nh, npr = (lax.axis_size(a) for a in ("blk", "head", "pair"))
    rows, width = single.shape
    half = rows // npr
    channels = pair.shape[3]
    heads = w_pair_bias.shape[1]
    size = w_query.shape[1] // heads
    queries = w_query_points.shape[1] // (3 * heads)
    values = w_kv_points.shape[1] // (3 * heads) - queries
    wide = up(heads * max(size, values), LANES)
    dims = (nb, nh, npr, heads, size, queries, values)
    vmem = pl.BlockSpec(memory_space=pltpu.VMEM)
    smem = pl.BlockSpec(memory_space=pltpu.SMEM)
    far = pl.BlockSpec(memory_space=pl.ANY)
    dma = pltpu.SemaphoreType.DMA
    flat = pair.reshape(rows * nb * half, channels)
    return tuple(
        pl.pallas_call(
            functools.partial(kernel, dims),
            out_shape=(
                jax.ShapeDtypeStruct((rows, width), jnp.bfloat16),
                jax.ShapeDtypeStruct((12, nb * rows), jnp.float32),
            ),
            in_specs=[
                vmem, far, vmem, vmem, vmem, smem, smem, vmem, vmem, vmem, vmem, vmem, smem, smem,
                far, vmem, vmem, vmem, vmem, vmem, vmem,
            ],
            out_specs=(vmem, vmem),
            scratch_shapes=[
                pltpu.VMEM((nb, half, width + LANES), jnp.float32),
                pltpu.VMEM((rows, LANES), jnp.float32),
                pltpu.VMEM(flat.shape, flat.dtype),
                pltpu.VMEM(w_out.shape, w_out.dtype),
                pltpu.VMEM((rows * SUB, channels), jnp.float32),
                pltpu.VMEM((npr, rows, LANES + 3 * wide), jnp.float32),
                pltpu.VMEM((nh * npr, rows, width), jnp.float32),
                pltpu.VMEM((nb, 16, rows), jnp.float32),
                dma((2,)),
                dma((nb,)),
                dma((nb,)),
                dma((npr,)),
                dma((npr,)),
                dma((nh * npr,)),
                dma((nh * npr,)),
                dma((nb,)),
                dma((nb,)),
            ],
            compiler_params=pltpu.CompilerParams(collective_id=0, has_side_effects=True),
        )(
            single, flat, frames, chain.reshape(1, rows), mask.reshape(1, rows), chain, mask,
            w_query, w_key_value, w_query_points, w_kv_points, w_pair_bias, head_weights,
            chain_bias, w_out, out_gain.reshape(1, width), w_backbone,
            *selectors(heads, size, queries, values),
        )
    )


def solution(mesh):
    placed = (
        P(("groups", "blk"), None),
        P(("groups", "blk"), None, "pair", None),
        P(None, ("groups", "blk")),
        P(("groups", "blk")),
        P(("groups", "blk")),
        P(None, "head"),
        P(None, "head"),
        P(None, "head"),
        P(None, "head"),
        P(None, "head"),
        P("head"),
        P("head"),
        P("head", None, None),
        P(),
        P(),
    )
    return jax.shard_map(
        body,
        mesh=mesh,
        in_specs=placed,
        out_specs=(P(("groups", "blk"), None), P(None, "groups")),
        check_vma=False,
    )
```

time: 86 us -> 35.1 us (0.41)
  blocking collectives: 31.6 us -> 0 us
  Pallas kernels: 0 us -> 25.2 us
  waiting for transfers between devices: 18.2 us -> 0 us
  matrix products: 9.58 us -> 0 us
  starting transfers between devices: 6.74 us -> 0 us
  local copies, waits for them, and re-layouts: 15 us -> 8.93 us
  other arithmetic: 2.83 us -> 0 us
    pallas_call x0 -> x1, Pallas kernels: none -> 25.2 us  [body(): pl.pallas_call(functools.partial(kernel, dims), out_shape=(jax.ShapeDtype...]
    all_gather x6 -> x0, blocking collectives: 23 us -> none  [the longest x1 13.1 us: body(): frames_out = lax.all_gather(frames_new, 'blk', axis=1, tiled=True)]
    ppermute x6 -> x0, waiting for transfers between devices: 18.2 us -> none  [shifted(): lax.ppermute(array, axis, [(i, (i + by) % peers) for i in range(peers)])]
    dot_general x30 -> x0, matrix products: 9.58 us -> none  [the longest x4 1.61 us: attention_logits(): jnp.dot(pair_rows.reshape(count_q * count_k, -1), w_pair_bias, preferred_...]
    psum x1 -> x0, blocking collectives: 8.59 us -> none  [body(): update = lax.psum(partial_update, 'head')]
    ppermute x6 -> x0, starting transfers between devices: 6.74 us -> none  [shifted(): lax.ppermute(array, axis, [(i, (i + by) % peers) for i in range(peers)])]
    while x20 -> x0, local copies, waits for them, and re-layouts: 2.45 us -> none
    slice x20 -> x0, local copies, waits for them, and re-layouts: 2.3 us -> none  [the longest x7 1.86 us: absorb(): points[:, :, query_count:]]
  transfers between devices with their start and end apart: 6 -> 0, of which waited for: 6 -> 0; matrix products, arithmetic and copies ran while one was open for 2% -> 0% of each run, Pallas kernels for 0% -> 0%
where the time goes in v1:
time: 35.1 us; the launch traced here: 34.8 us
  Pallas kernels  25.2 us (72%)
  local copies, waits for them, and re-layouts  8.93 us (25%)
  between operations  0.66 us (2%)
    pallas_call x1, Pallas kernels, body(): pl.pallas_call(functools.partial(kernel, dims), out_shape=(jax.ShapeDtype...  25.2 us
    unnamed x22, local copies, waits for them, and re-layouts  8.36 us

profile of v1, /device:TPU:0, one launch (start us, length us, event | category | flops | bytes accessed | tf_op | source)
XLA Modules:
  0.0 34.8 jit_solution(18012482583566280015)
XLA Ops:
  0.6 0.0 copy-start.6
  0.6 0.7 %copy-done.6 = f32[384]{0:T(512)S(1)} copy-done((f32[384]{0:T(512)S(1)}, f32[384]{0:T(512)}, u32[]{:S(2)}) %copy-start.6) | copy-done | bytes 1560
  1.3 0.0 copy-start.5
  1.3 0.6 %reshape.19.gain_ref = f32[1,384]{1,0:T(1,128)} reshape(f32[384]{0:T(512)S(1)} %copy-done.6) | data formatting | bytes 3072 | tf_op jit(solution)/shard_map/reshape | solution.py:421
  1.9 0.1 copy-done.5
  2.0 0.7 %copy.25.wpb_ref = bf16[128,6]{1,0:T(8,128)(2,1)} copy(bf16[128,6]{0,1:T(8,128)(2,1)S(1)} %copy-done.5) | data formatting | bytes 3072 | tf_op args[9]
  2.7 0.0 copy-start.2
  2.7 1.6 %copy.21.wq_ref = bf16[384,96]{1,0:T(8,128)(2,1)} copy(bf16[384,96]{0,1:T(8,128)(2,1)} %param.24) | data formatting | bytes 147456 | tf_op args[5]
  4.3 0.0 copy-done.2
  4.4 0.0 copy-start.4
  4.4 0.0 copy-start.1
  4.4 0.7 %copy.23.wqp_ref = bf16[384,72]{1,0:T(8,128)(2,1)} copy(bf16[384,72]{0,1:T(8,128)(2,1)S(1)} %copy-done.2) | data formatting | bytes 110592 | tf_op args[7]
  5.1 0.0 copy-done.4
  5.1 0.8 %copy.26.wbb_ref = bf16[384,6]{1,0:T(8,128)(2,1)} copy(bf16[384,6]{0,1:T(8,128)(2,1)S(1)} %copy-done.4) | data formatting | bytes 9216 | tf_op args[14]
  5.9 0.0 copy-done.1
  5.9 0.0 copy-start
  5.9 0.8 %copy.22.wkv_ref = bf16[384,192]{1,0:T(8,128)(2,1)} copy(bf16[384,192]{0,1:T(8,128)(2,1)S(1)} %copy-done.1) | data formatting | bytes 294912 | tf_op args[6]
  6.7 0.1 copy-done
  6.8 0.8 %copy.24.wkp_ref = bf16[384,216]{1,0:T(8,128)(2,1)} copy(bf16[384,216]{0,1:T(8,128)(2,1)S(1)} %copy-done) | data formatting | bytes 331776 | tf_op args[8]
  7.6 25.2 %shard_map.194 = (bf16[32,384]{1,0:T(8,128)(2,1)}, f32[12,128]{1,0:T(8,128)}) custom-call(bf16[32,384]{1,0:T(8,128)(2,1)} %single_ref.1, bf16[2048,128]{1,0:T(8,128)(2,1)} %bitcast.3, f32[12,32]{1,0:T(8,128)} %frames_ref.1, s32[1,32]{1,0:T(1,128)} %bitcast.4, s32[1,32]{1,0:T(1,128)} %bitcast.5, s32[32]{0:T(128)} %chain_ref.1, s32[32]{0:T(128)} %mask_ref.1, ...), custom_call_target="tpu_custom_call" | custom-call | tf_op jit(solution)/shard_map/pallas_call | solution.py:387
  32.8 0.0 copy-start.3
  32.8 1.4 %copy.29 = bf16[32,384]{1,0:T(8,128)(2,1)} copy(bf16[32,384]{1,0:T(8,128)(2,1)} %get-tuple-element.4) | data formatting | bytes 49152
  34.2 0.0 copy-done.3
  34.2 0.6 %copy.30 = f32[12,128]{1,0:T(8,128)} copy(f32[12,128]{1,0:T(8,128)S(1)} %copy-done.3) | data formatting | bytes 12288
Async XLA Ops:
  0.6 0.7 %copy-start.6 = (f32[384]{0:T(512)S(1)}, f32[384]{0:T(512)}, u32[]{:S(2)}) copy-start(f32[384]{0:T(512)} %param.32) | copy-start | bytes 4612
  1.3 0.7 %copy-start.5 = (bf16[128,6]{0,1:T(8,128)(2,1)S(1)}, bf16[128,6]{0,1:T(8,128)(2,1)}, u32[]{:S(2)}) copy-start(bf16[128,6]{0,1:T(8,128)(2,1)} %param.28) | copy-start | bytes 4612
  2.7 1.6 %copy-start.2 = (bf16[384,72]{0,1:T(8,128)(2,1)S(1)}, bf16[384,72]{0,1:T(8,128)(2,1)}, u32[]{:S(2)}) copy-start(bf16[384,72]{0,1:T(8,128)(2,1)} %param.26) | copy-start | bytes 165892
  4.4 0.7 %copy-start.4 = (bf16[384,6]{0,1:T(8,128)(2,1)S(1)}, bf16[384,6]{0,1:T(8,128)(2,1)}, u32[]{:S(2)}) copy-start(bf16[384,6]{0,1:T(8,128)(2,1)} %param.33) | copy-start | bytes 13828
  4.4 1.5 %copy-start.1 = (bf16[384,192]{0,1:T(8,128)(2,1)S(1)}, bf16[384,192]{0,1:T(8,128)(2,1)}, u32[]{:S(2)}) copy-start(bf16[384,192]{0,1:T(8,128)(2,1)} %param.25) | copy-start | bytes 442372
  5.9 0.9 %copy-start = (bf16[384,216]{0,1:T(8,128)(2,1)S(1)}, bf16[384,216]{0,1:T(8,128)(2,1)}, u32[]{:S(2)}) copy-start(bf16[384,216]{0,1:T(8,128)(2,1)} %param.27) | copy-start | bytes 497668
  32.8 1.4 %copy-start.3 = (f32[12,128]{1,0:T(8,128)S(1)}, f32[12,128]{1,0:T(8,128)}, u32[]{:S(2)}) copy-start(f32[12,128]{1,0:T(8,128)} %get-tuple-element.5) | copy-start | bytes 18436

commit v2 on v1

--- a/solution.py
+++ b/solution.py
@@ -118,8 +118,8 @@
     gath[me_b, :, width:] = meta_s[pl.ds(start, half), :]
 
     single = single_ref[...]
-    w_kv = nt(selkv_ref[...], wkv_ref[...]).astype(bf16)
-    w_kp = nt(selkp_ref[...], wkp_ref[...]).astype(bf16)
+    w_kv = nn(selkv_ref[...], wkv_ref[...]).astype(bf16)
+    w_kp = nn(selkp_ref[...], wkp_ref[...]).astype(bf16)
 
     pl.semaphore_wait(barrier, nb - 1 + len(group))
     gathers = []
@@ -135,8 +135,8 @@
         copy.start()
         gathers.append(copy)
 
-    w_qp = nt(selq_ref[...], wqp_ref[...]).astype(bf16)
-    query = nn(single, wq_ref[...]) * (1.0 / math.sqrt(size))
+    w_qp = nn(selq_ref[...], wqp_ref[...]).astype(bf16)
+    query = nt(single, wq_ref[...]) * (1.0 / math.sqrt(size))
     q_local = nt(w_qp, single)
     step = queries * SUB
 
@@ -156,12 +156,12 @@
         lax.broadcasted_iota(jnp.int32, (SUB, heads), 0)
         == lax.broadcasted_iota(jnp.int32, (SUB, heads), 1)
     ).astype(bf16)
-    w_bias = nt(eye, wpb_ref[...]).astype(bf16)
+    w_bias = nn(eye, wpb_ref[...]).astype(bf16)
     eye6 = (
-        lax.broadcasted_iota(jnp.int32, (SUB, wbb_ref.shape[1]), 0)
-        == lax.broadcasted_iota(jnp.int32, (SUB, wbb_ref.shape[1]), 1)
+        lax.broadcasted_iota(jnp.int32, (SUB, wbb_ref.shape[0]), 0)
+        == lax.broadcasted_iota(jnp.int32, (SUB, wbb_ref.shape[0]), 1)
     ).astype(bf16)
-    w_back = nt(eye6, wbb_ref[...]).astype(bf16)
+    w_back = nn(eye6, wbb_ref[...]).astype(bf16)
     head_row = lax.broadcasted_iota(jnp.int32, (SUB, keys), 0)
     raw = jnp.zeros((SUB, keys), f32)
     chain_term = jnp.zeros((SUB, keys), f32)
@@ -321,7 +321,7 @@
     centre = jnp.mean(mixed, axis=1, keepdims=True)
     away = mixed - centre
     variance = jnp.mean(away * away, axis=1, keepdims=True)
-    out = (away * lax.rsqrt(variance + 1e-05) * gain_ref[...]).astype(bf16)
+    out = (away * lax.rsqrt(variance + 1e-05) * gain_ref[...].reshape(1, width)).astype(bf16)
     so_ref[...] = out
     motion = nt(w_back, out)
     m = [motion[k : k + 1] for k in range(6)]
@@ -417,8 +417,8 @@
             compiler_params=pltpu.CompilerParams(collective_id=0, has_side_effects=True),
         )(
             single, flat, frames, chain.reshape(1, rows), mask.reshape(1, rows), chain, mask,
-            w_query, w_key_value, w_query_points, w_kv_points, w_pair_bias, head_weights,
-            chain_bias, w_out, out_gain.reshape(1, width), w_backbone,
+            w_query.T, w_key_value.T, w_query_points.T, w_kv_points.T, w_pair_bias.T, head_weights,
+            chain_bias, w_out, out_gain, w_backbone.T,
             *selectors(heads, size, queries, values),
         )
     )

time: 35.1 us -> 27.9 us (0.79)
  local copies, waits for them, and re-layouts: 8.93 us -> 1.96 us
    unnamed x22 -> x4, local copies, waits for them, and re-layouts: 8.36 us -> 1.96 us
    reshape x1 -> x0, local copies, waits for them, and re-layouts: 0.56 us -> none  [body(): out_gain.reshape(1, width)]
where the time goes in v2:
time: 27.9 us; the launch traced here: 27.7 us
  Pallas kernels  25.1 us (90%)
  local copies, waits for them, and re-layouts  1.96 us (7%)
  between operations  0.65 us (2%)
    pallas_call x1, Pallas kernels, body(): pl.pallas_call(functools.partial(kernel, dims), out_shape=(jax.ShapeDtype...  25.1 us
    unnamed x4, local copies, waits for them, and re-layouts  1.96 us

profile of v2, /device:TPU:0, one launch (start us, length us, event | category | flops | bytes accessed | tf_op | source)
XLA Modules:
  0.0 27.7 jit_solution(3334310384251536840)
XLA Ops:
  0.6 25.1 %shard_map.194 = (bf16[32,384]{1,0:T(8,128)(2,1)}, f32[12,128]{1,0:T(8,128)}) custom-call(bf16[32,384]{1,0:T(8,128)(2,1)} %single_ref.1, bf16[2048,128]{1,0:T(8,128)(2,1)} %bitcast.9, f32[12,32]{1,0:T(8,128)} %frames_ref.1, s32[1,32]{1,0:T(1,128)} %bitcast.16, s32[1,32]{1,0:T(1,128)} %bitcast.17, s32[32]{0:T(128)} %chain_ref.1, s32[32]{0:T(128)} %mask_ref.1, ...), custom_call_target="tpu_custom_call" | custom-call | tf_op jit(solution)/shard_map/pallas_call | solution.py:387
  25.8 0.0 copy-start
  25.8 1.4 %copy.23 = bf16[32,384]{1,0:T(8,128)(2,1)} copy(bf16[32,384]{1,0:T(8,128)(2,1)} %get-tuple-element.4) | data formatting | bytes 49152
  27.1 0.0 copy-done
  27.1 0.6 %copy.24 = f32[12,128]{1,0:T(8,128)} copy(f32[12,128]{1,0:T(8,128)S(1)} %copy-done) | data formatting | bytes 12288
Async XLA Ops:
  25.8 1.4 %copy-start = (f32[12,128]{1,0:T(8,128)S(1)}, f32[12,128]{1,0:T(8,128)}, u32[]{:S(2)}) copy-start(f32[12,128]{1,0:T(8,128)} %get-tuple-element.5) | copy-start | bytes 18436

commit v3 on v2

--- a/solution.py
+++ b/solution.py
@@ -66,17 +66,36 @@
     return [jnp.asarray(s, jnp.bfloat16) for s in (sel_q, sel_kv, sel_kp, sel_out)]
 
 
-def kernel(
-    dims,
-    single_ref, pair_hbm, frames_ref, chain_row_ref, mask_row_ref, chain_ref, mask_ref,
-    wq_ref, wkv_ref, wqp_ref, wkp_ref, wpb_ref, hw_ref, cb_ref, wout_hbm, gain_ref, wbb_ref,
-    selq_ref, selkv_ref, selkp_ref, selout_ref,
-    so_ref, fo_ref,
-    gath, meta_s, pair_v, wout_v, sp, ex, red, fg,
-    load_sem, gs_sem, gr_sem, es_sem, er_sem, rs_sem, rr_sem, fs_sem, fr_sem,
-):
+ORDER = (
+    "frames", "chain_row", "mask_row", "single", "sel_kv", "w_kv", "sel_kp", "w_kp", "sel_q", "w_qp",
+    "w_q", "w_bias", "w_back", "head_weights", "chain_bias", "pair", "w_out", "sel_out", "chain",
+    "mask", "gain",
+)
+SCALARS = ("head_weights", "chain_bias", "chain", "mask")
+
+
+def kernel(dims, *refs):
+    count = len(ORDER)
+    far = refs[:count]
+    so_ref, fo_ref = refs[count : count + 2]
+    near = dict(zip(ORDER, refs[count + 2 : 2 * count + 2]))
+    (
+        gath, meta_s, sp, ex, red, fg,
+        load_sem, gs_sem, gr_sem, es_sem, er_sem, rs_sem, rr_sem, fs_sem, fr_sem,
+    ) = refs[2 * count + 2 :]
+    loads = {
+        name: pltpu.make_async_copy(source, near[name], load_sem.at[k])
+        for k, (name, source) in enumerate(zip(ORDER, far))
+    }
+    for name in ORDER:
+        loads[name].start()
+
+    def loaded(name):
+        loads[name].wait()
+        return near[name]
+
     nb, nh, npr, heads, size, queries, values = dims
-    rows, width = single_ref.shape
+    rows, width = near["single"].shape
     half = rows // npr
     keys = nb * half
     wide = up(heads * max(size, values), LANES)
@@ -92,22 +111,21 @@
         return {"head": lax.rem(me_h + dh, nh), "pair": lax.rem(me_p + dp, npr)}
 
     group = [(dh, dp) for dh in range(nh) for dp in range(npr) if dh or dp]
-    load_pair = pltpu.make_async_copy(pair_hbm, pair_v, load_sem.at[0])
-    load_pair.start()
-    load_out = pltpu.make_async_copy(wout_hbm, wout_v, load_sem.at[1])
-    load_out.start()
     barrier = pltpu.get_barrier_semaphore()
     for d in range(1, nb):
         pl.semaphore_signal(barrier, inc=1, device_id=blk_peer(d), device_id_type=MESH)
     for dh, dp in group:
         pl.semaphore_signal(barrier, inc=1, device_id=group_peer(dh, dp), device_id_type=MESH)
 
-    frames = frames_ref[...]
+    frames = loaded("frames")[...]
+    chain_row = loaded("chain_row")[...].astype(f32)
+    mask_row = loaded("mask_row")[...].astype(f32)
+    single_ref = loaded("single")
     meta = jnp.concatenate(
         [
             frames,
-            chain_row_ref[...].astype(f32),
-            mask_row_ref[...].astype(f32),
+            chain_row,
+            mask_row,
             jnp.zeros((LANES - 14, rows), f32),
         ],
         axis=0,
@@ -118,9 +136,6 @@
     gath[me_b, :, width:] = meta_s[pl.ds(start, half), :]
 
     single = single_ref[...]
-    w_kv = nn(selkv_ref[...], wkv_ref[...]).astype(bf16)
-    w_kp = nn(selkp_ref[...], wkp_ref[...]).astype(bf16)
-
     pl.semaphore_wait(barrier, nb - 1 + len(group))
     gathers = []
     for d in range(1, nb):
@@ -135,8 +150,10 @@
         copy.start()
         gathers.append(copy)
 
-    w_qp = nn(selq_ref[...], wqp_ref[...]).astype(bf16)
-    query = nt(single, wq_ref[...]) * (1.0 / math.sqrt(size))
+    w_kv = nn(loaded("sel_kv")[...], loaded("w_kv")[...]).astype(bf16)
+    w_kp = nn(loaded("sel_kp")[...], loaded("w_kp")[...]).astype(bf16)
+    w_qp = nn(loaded("sel_q")[...], loaded("w_qp")[...]).astype(bf16)
+    query = nt(single, loaded("w_q")[...]) * (1.0 / math.sqrt(size))
     q_local = nt(w_qp, single)
     step = queries * SUB
 
@@ -156,7 +173,8 @@
         lax.broadcasted_iota(jnp.int32, (SUB, heads), 0)
         == lax.broadcasted_iota(jnp.int32, (SUB, heads), 1)
     ).astype(bf16)
-    w_bias = nn(eye, wpb_ref[...]).astype(bf16)
+    w_bias = nn(eye, loaded("w_bias")[...]).astype(bf16)
+    wbb_ref = loaded("w_back")
     eye6 = (
         lax.broadcasted_iota(jnp.int32, (SUB, wbb_ref.shape[0]), 0)
         == lax.broadcasted_iota(jnp.int32, (SUB, wbb_ref.shape[0]), 1)
@@ -165,6 +183,7 @@
     head_row = lax.broadcasted_iota(jnp.int32, (SUB, keys), 0)
     raw = jnp.zeros((SUB, keys), f32)
     chain_term = jnp.zeros((SUB, keys), f32)
+    hw_ref, cb_ref = loaded("head_weights"), loaded("chain_bias")
     for h in range(heads):
         raw = jnp.where(head_row == h, hw_ref[h], raw)
         chain_term = jnp.where(head_row == h, cb_ref[h], chain_term)
@@ -175,13 +194,13 @@
         == lax.broadcasted_iota(jnp.int32, (SUB, heads * size), 0)
     ).astype(f32)
     q_wide = (query[:, None, :] * own_head[None]).reshape(rows * SUB, heads * size)
-    load_pair.wait()
+    pair_v = loaded("pair")
     pairs = [pair_v[i * keys : (i + 1) * keys, :] for i in range(rows)]
     biases = [nt(w_bias, pairs[i]) for i in range(rows)]
-    load_out.wait()
+    wout_v = loaded("w_out")
     small = size + 4 * values
     w_small = nn(
-        selout_ref[...], jnp.concatenate([wout_v[h, :small, :] for h in range(heads)], axis=0)
+        loaded("sel_out")[...], jnp.concatenate([wout_v[h, :small, :] for h in range(heads)], axis=0)
     ).astype(bf16)
 
     for copy in gathers:
@@ -197,6 +216,7 @@
     dots = dot3(nn, q_wide, kv[: heads * size])
     key_chain = jnp.broadcast_to(key_meta[12:13], (SUB, keys))
     key_present = jnp.broadcast_to(key_meta[13:14], (SUB, keys))
+    chain_ref, mask_ref = loaded("chain"), loaded("mask")
 
     weights, tops, totals = [], [], []
     for i in range(rows):
@@ -321,7 +341,7 @@
     centre = jnp.mean(mixed, axis=1, keepdims=True)
     away = mixed - centre
     variance = jnp.mean(away * away, axis=1, keepdims=True)
-    out = (away * lax.rsqrt(variance + 1e-05) * gain_ref[...].reshape(1, width)).astype(bf16)
+    out = (away * lax.rsqrt(variance + 1e-05) * loaded("gain")[...].reshape(1, width)).astype(bf16)
     so_ref[...] = out
     motion = nt(w_back, out)
     m = [motion[k : k + 1] for k in range(6)]
@@ -345,7 +365,8 @@
     lines += [
         turn[9 + a] + sum(turn[3 * a + b] * m[3 + b] for b in range(3)) for a in range(3)
     ]
-    fg[me_b] = jnp.concatenate(lines + [jnp.zeros((4, rows), f32)], axis=0)
+    lines = jnp.concatenate(lines + [jnp.zeros((4, rows), f32)], axis=0)
+    fg[me_b] = jnp.concatenate([lines, jnp.zeros((16, LANES - rows), f32)], axis=1)
     finals = []
     for d in range(1, nb):
         copy = pltpu.make_async_remote_copy(
@@ -361,7 +382,7 @@
     for copy in finals:
         copy.wait()
     for k in range(nb):
-        fo_ref[:, k * rows : (k + 1) * rows] = fg[k, :12, :]
+        fo_ref[:, k * rows : (k + 1) * rows] = fg[k, :12, :rows]
 
 
 def body(
@@ -379,10 +400,21 @@
     wide = up(heads * max(size, values), LANES)
     dims = (nb, nh, npr, heads, size, queries, values)
     vmem = pl.BlockSpec(memory_space=pltpu.VMEM)
-    smem = pl.BlockSpec(memory_space=pltpu.SMEM)
-    far = pl.BlockSpec(memory_space=pl.ANY)
     dma = pltpu.SemaphoreType.DMA
-    flat = pair.reshape(rows * nb * half, channels)
+    selected = selectors(heads, size, queries, values)
+    given = dict(zip(("sel_q", "sel_kv", "sel_kp", "sel_out"), selected))
+    given.update(
+        single=single, pair=pair.reshape(rows * nb * half, channels), frames=frames,
+        chain_row=chain.reshape(1, rows), mask_row=mask.reshape(1, rows), chain=chain, mask=mask,
+        w_q=w_query.T, w_kv=w_key_value.T, w_qp=w_query_points.T, w_kp=w_kv_points.T,
+        w_bias=w_pair_bias.T, head_weights=head_weights, chain_bias=chain_bias, w_out=w_out,
+        gain=out_gain, w_back=w_backbone.T,
+    )
+    operands = [given[name] for name in ORDER]
+    held = [
+        (pltpu.SMEM if name in SCALARS else pltpu.VMEM)(given[name].shape, given[name].dtype)
+        for name in ORDER
+    ]
     return tuple(
         pl.pallas_call(
             functools.partial(kernel, dims),
@@ -390,21 +422,17 @@
                 jax.ShapeDtypeStruct((rows, width), jnp.bfloat16),
                 jax.ShapeDtypeStruct((12, nb * rows), jnp.float32),
             ),
-            in_specs=[
-                vmem, far, vmem, vmem, vmem, smem, smem, vmem, vmem, vmem, vmem, vmem, smem, smem,
-                far, vmem, vmem, vmem, vmem, vmem, vmem,
-            ],
+            in_specs=[pl.BlockSpec(memory_space=pl.ANY)] * len(operands),
             out_specs=(vmem, vmem),
-            scratch_shapes=[
+            scratch_shapes=held
+            + [
                 pltpu.VMEM((nb, half, width + LANES), jnp.float32),
                 pltpu.VMEM((rows, LANES), jnp.float32),
-                pltpu.VMEM(flat.shape, flat.dtype),
-                pltpu.VMEM(w_out.shape, w_out.dtype),
                 pltpu.VMEM((rows * SUB, channels), jnp.float32),
                 pltpu.VMEM((npr, rows, LANES + 3 * wide), jnp.float32),
                 pltpu.VMEM((nh * npr, rows, width), jnp.float32),
-                pltpu.VMEM((nb, 16, rows), jnp.float32),
-                dma((2,)),
+                pltpu.VMEM((nb, 16, LANES), jnp.float32),
+                dma((len(operands),)),
                 dma((nb,)),
                 dma((nb,)),
                 dma((npr,)),
@@ -415,12 +443,7 @@
                 dma((nb,)),
             ],
             compiler_params=pltpu.CompilerParams(collective_id=0, has_side_effects=True),
-        )(
-            single, flat, frames, chain.reshape(1, rows), mask.reshape(1, rows), chain, mask,
-            w_query.T, w_key_value.T, w_query_points.T, w_kv_points.T, w_pair_bias.T, head_weights,
-            chain_bias, w_out, out_gain, w_backbone.T,
-            *selectors(heads, size, queries, values),
-        )
+        )(*operands)
     )
 
 

time: 27.9 us -> 28.1 us (level)
  no operation moved by 1% of the time
where the time goes in v3:
time: 28.1 us; the launch traced here: 27.9 us
  Pallas kernels  25.3 us (90%)
  local copies, waits for them, and re-layouts  1.96 us (7%)
  between operations  0.65 us (2%)
    pallas_call x1, Pallas kernels, body(): pl.pallas_call(functools.partial(kernel, dims), out_shape=(jax.ShapeDtype...  25.3 us
    unnamed x4, local copies, waits for them, and re-layouts  1.96 us

profile of v3, /device:TPU:0, one launch (start us, length us, event | category | flops | bytes accessed | tf_op | source)
XLA Modules:
  0.0 27.9 jit_solution(16245418979802034874)
XLA Ops:
  0.6 25.3 %shard_map.194 = (bf16[32,384]{1,0:T(8,128)(2,1)}, f32[12,128]{1,0:T(8,128)}) custom-call(f32[12,32]{1,0:T(8,128)} %refs_0_.1, s32[1,32]{1,0:T(1,128)} %bitcast.16, s32[1,32]{1,0:T(1,128)} %bitcast.17, bf16[32,384]{1,0:T(8,128)(2,1)} %refs_3_.1, bf16[224,192]{1,0:T(8,128)(2,1)} %constant.9.clone.refs_4_, bf16[192,384]{1,0:T(8,128)(2,1)} %bitcast.11, ...), custom_call_target="tpu_custom_call" | custom-call | tf_op jit(solution)/shard_map/pallas_call | solution.py:419
  25.9 0.0 copy-start
  25.9 1.4 %copy.23 = bf16[32,384]{1,0:T(8,128)(2,1)} copy(bf16[32,384]{1,0:T(8,128)(2,1)} %get-tuple-element.4) | data formatting | bytes 49152
  27.3 0.0 copy-done
  27.3 0.6 %copy.24 = f32[12,128]{1,0:T(8,128)} copy(f32[12,128]{1,0:T(8,128)S(1)} %copy-done) | data formatting | bytes 12288
Async XLA Ops:
  25.9 1.4 %copy-start = (f32[12,128]{1,0:T(8,128)S(1)}, f32[12,128]{1,0:T(8,128)}, u32[]{:S(2)}) copy-start(f32[12,128]{1,0:T(8,128)} %get-tuple-element.5) | copy-start | bytes 18436

commit v4 on v3

--- a/solution.py
+++ b/solution.py
@@ -80,15 +80,14 @@
     so_ref, fo_ref = refs[count : count + 2]
     near = dict(zip(ORDER, refs[count + 2 : 2 * count + 2]))
     (
-        gath, meta_s, sp, ex, red, fg,
+        gath, meta_s, sp, ex, part, red, so32, fg,
         load_sem, gs_sem, gr_sem, es_sem, er_sem, rs_sem, rr_sem, fs_sem, fr_sem,
+        os_sem, or_sem,
     ) = refs[2 * count + 2 :]
     loads = {
         name: pltpu.make_async_copy(source, near[name], load_sem.at[k])
         for k, (name, source) in enumerate(zip(ORDER, far))
     }
-    for name in ORDER:
-        loads[name].start()
 
     def loaded(name):
         loads[name].wait()
@@ -104,19 +103,19 @@
     me_p = lax.axis_index("pair")
     f32, bf16 = jnp.float32, jnp.bfloat16
 
-    def blk_peer(d):
-        return {"blk": lax.rem(me_b + d, nb)}
+    def block_peer(d, dp):
+        return {"blk": lax.rem(me_b + d, nb), "pair": lax.rem(me_p + dp, npr)}
 
     def group_peer(dh, dp):
         return {"head": lax.rem(me_h + dh, nh), "pair": lax.rem(me_p + dp, npr)}
 
+    block = [(d, dp) for d in range(nb) for dp in range(npr) if d or dp]
     group = [(dh, dp) for dh in range(nh) for dp in range(npr) if dh or dp]
     barrier = pltpu.get_barrier_semaphore()
-    for d in range(1, nb):
-        pl.semaphore_signal(barrier, inc=1, device_id=blk_peer(d), device_id_type=MESH)
-    for dh, dp in group:
-        pl.semaphore_signal(barrier, inc=1, device_id=group_peer(dh, dp), device_id_type=MESH)
-
+    for peer in [block_peer(d, dp) for d, dp in block] + [group_peer(dh, dp) for dh, dp in group if dh]:
+        pl.semaphore_signal(barrier, inc=1, device_id=peer, device_id_type=MESH)
+    for name in ORDER:
+        loads[name].start()
     frames = loaded("frames")[...]
     chain_row = loaded("chain_row")[...].astype(f32)
     mask_row = loaded("mask_row")[...].astype(f32)
@@ -134,21 +133,34 @@
     start = pl.multiple_of(me_p * half, half)
     gath[me_b, :, :width] = single_ref[pl.ds(start, half), :].astype(f32)
     gath[me_b, :, width:] = meta_s[pl.ds(start, half), :]
+    my_frames = meta_s[pl.ds(start, half), :].T
 
     single = single_ref[...]
-    pl.semaphore_wait(barrier, nb - 1 + len(group))
+    pl.semaphore_wait(barrier, len(block) + (nh - 1) * npr)
     gathers = []
-    for d in range(1, nb):
+    upper = (2 * me_b) // nb
+    for s in range(nb - 1):
+        rising = s + (s - me_b + nb) // nb
+        falling = nb - 1 - s - (me_b - (nb - 1 - s) + nb) // nb
+        peer = upper * rising + (1 - upper) * falling
         copy = pltpu.make_async_remote_copy(
             src_ref=gath.at[me_b],
             dst_ref=gath.at[me_b],
-            send_sem=gs_sem.at[d],
-            recv_sem=gr_sem.at[d],
-            device_id=blk_peer(d),
+            send_sem=gs_sem.at[s],
+            recv_sem=gr_sem.at[me_b],
+            device_id={"blk": peer},
             device_id_type=MESH,
         )
         copy.start()
-        gathers.append(copy)
+        landing = pltpu.make_async_remote_copy(
+            src_ref=gath.at[peer],
+            dst_ref=gath.at[peer],
+            send_sem=gs_sem.at[s],
+            recv_sem=gr_sem.at[peer],
+            device_id={"blk": peer},
+            device_id_type=MESH,
+        )
+        gathers.append((copy, landing))
 
     w_kv = nn(loaded("sel_kv")[...], loaded("w_kv")[...]).astype(bf16)
     w_kp = nn(loaded("sel_kp")[...], loaded("w_kp")[...]).astype(bf16)
@@ -203,8 +215,8 @@
         loaded("sel_out")[...], jnp.concatenate([wout_v[h, :small, :] for h in range(heads)], axis=0)
     ).astype(bf16)
 
-    for copy in gathers:
-        copy.wait()
+    for copy, landing in gathers:
+        landing.wait_recv()
     everyone = gath[...].reshape(keys, width + LANES)
     key_single = everyone[:, :width].astype(bf16)
     key_meta = everyone[:, width:].T
@@ -316,12 +328,13 @@
     for h in range(heads):
         paired = sp[pl.ds(h, rows, stride=SUB), :] * factors[0][:, h : h + 1]
         partial = partial + nn(paired.astype(bf16), wout_v[h, small:, :])
-    red[0] = partial
+    part[...] = partial
     reductions = []
     for dh, dp in group:
         code = dh * npr + dp
+        target = pl.multiple_of(lax.rem(me_p + dp, npr) * half, half)
         copy = pltpu.make_async_remote_copy(
-            src_ref=red.at[0],
+            src_ref=part.at[pl.ds(target, half)],
             dst_ref=red.at[code],
             send_sem=rs_sem.at[code],
             recv_sem=rr_sem.at[code],
@@ -330,19 +343,21 @@
         )
         copy.start()
         reductions.append(copy)
+    red[0] = part[pl.ds(start, half), :]
+    for copy, landing in gathers:
+        copy.wait_send()
     for copy in reductions:
         copy.wait()
-    update = jnp.zeros((rows, width), f32)
+    update = jnp.zeros((half, width), f32)
     for h in range(nh):
         for p in range(npr):
             code = lax.rem(me_h - h + nh, nh) * npr + lax.rem(me_p - p + npr, npr)
             update = update + red[code]
-    mixed = single.astype(f32) + update
+    mixed = gath[me_b, :, :width] + update
     centre = jnp.mean(mixed, axis=1, keepdims=True)
     away = mixed - centre
     variance = jnp.mean(away * away, axis=1, keepdims=True)
     out = (away * lax.rsqrt(variance + 1e-05) * loaded("gain")[...].reshape(1, width)).astype(bf16)
-    so_ref[...] = out
     motion = nt(w_back, out)
     m = [motion[k : k + 1] for k in range(6)]
     inverse = 1.0 / jnp.sqrt(1.0 + m[0] * m[0] + m[1] * m[1] + m[2] * m[2])
@@ -358,31 +373,50 @@
         2.0 * (qc * qd + qa * qb),
         qa * qa - qb * qb - qc * qc + qd * qd,
     ]
-    turn = [frames[k : k + 1] for k in range(12)]
+    turn = [my_frames[k : k + 1] for k in range(12)]
     lines = [
         sum(turn[3 * a + b] * spin[3 * b + c] for b in range(3)) for a in range(3) for c in range(3)
     ]
     lines += [
         turn[9 + a] + sum(turn[3 * a + b] * m[3 + b] for b in range(3)) for a in range(3)
     ]
-    lines = jnp.concatenate(lines + [jnp.zeros((4, rows), f32)], axis=0)
-    fg[me_b] = jnp.concatenate([lines, jnp.zeros((16, LANES - rows), f32)], axis=1)
+    lines = jnp.concatenate(lines + [jnp.zeros((4, half), f32)], axis=0)
+    fg[me_b, me_p] = jnp.concatenate([lines, jnp.zeros((16, LANES - half), f32)], axis=1)
     finals = []
-    for d in range(1, nb):
+    for d, dp in block:
+        code = d * npr + dp
         copy = pltpu.make_async_remote_copy(
-            src_ref=fg.at[me_b],
-            dst_ref=fg.at[me_b],
-            send_sem=fs_sem.at[d],
-            recv_sem=fr_sem.at[d],
-            device_id=blk_peer(d),
+            src_ref=fg.at[me_b, me_p],
+            dst_ref=fg.at[me_b, me_p],
+            send_sem=fs_sem.at[code],
+            recv_sem=fr_sem.at[code],
+            device_id=block_peer(d, dp),
             device_id_type=MESH,
         )
         copy.start()
         finals.append(copy)
-    for copy in finals:
+    so32[me_p] = out.astype(f32)
+    for d in range(1, npr):
+        copy = pltpu.make_async_remote_copy(
+            src_ref=so32.at[me_p],
+            dst_ref=so32.at[me_p],
+            send_sem=os_sem.at[d],
+            recv_sem=or_sem.at[d],
+            device_id=group_peer(0, d),
+            device_id_type=MESH,
+        )
+        copy.start()
+        finals.append(copy)
+    for copy in finals[len(block) :]:
+        copy.wait()
+    for p in range(npr):
+        so_ref[p * half : (p + 1) * half, :] = so32[p].astype(bf16)
+    for copy in finals[: len(block)]:
         copy.wait()
     for k in range(nb):
-        fo_ref[:, k * rows : (k + 1) * rows] = fg[k, :12, :rows]
+        for p in range(npr):
+            spot = (k * npr + p) * half
+            fo_ref[:, spot : spot + half] = fg[k, p, :12, :half]
 
 
 def body(
@@ -430,8 +464,10 @@
                 pltpu.VMEM((rows, LANES), jnp.float32),
                 pltpu.VMEM((rows * SUB, channels), jnp.float32),
                 pltpu.VMEM((npr, rows, LANES + 3 * wide), jnp.float32),
-                pltpu.VMEM((nh * npr, rows, width), jnp.float32),
-                pltpu.VMEM((nb, 16, LANES), jnp.float32),
+                pltpu.VMEM((rows, width), jnp.float32),
+                pltpu.VMEM((nh * npr, half, width), jnp.float32),
+                pltpu.VMEM((npr, half, width), jnp.float32),
+                pltpu.VMEM((nb, npr, 16, LANES), jnp.float32),
                 dma((len(operands),)),
                 dma((nb,)),
                 dma((nb,)),
@@ -439,8 +475,10 @@
                 dma((npr,)),
                 dma((nh * npr,)),
                 dma((nh * npr,)),
-                dma((nb,)),
-                dma((nb,)),
+                dma((nb * npr,)),
+                dma((nb * npr,)),
+                dma((npr,)),
+                dma((npr,)),
             ],
             compiler_params=pltpu.CompilerParams(collective_id=0, has_side_effects=True),
         )(*operands)

time: 28.1 us -> 26.7 us (0.950)
  Pallas kernels: 25.3 us -> 23.9 us
    pallas_call x1, Pallas kernels: 25.3 us -> 23.9 us  [body(): pl.pallas_call(functools.partial(kernel, dims), out_shape=(jax.ShapeDtype...]
where the time goes in v4:
time: 26.7 us; the launch traced here: 26.5 us
  Pallas kernels  23.9 us (90%)
  local copies, waits for them, and re-layouts  1.96 us (7%)
  between operations  0.65 us (2%)
    pallas_call x1, Pallas kernels, body(): pl.pallas_call(functools.partial(kernel, dims), out_shape=(jax.ShapeDtype...  23.9 us
    unnamed x4, local copies, waits for them, and re-layouts  1.96 us

profile of v4, /device:TPU:0, one launch (start us, length us, event | category | flops | bytes accessed | tf_op | source)
XLA Modules:
  0.0 26.5 jit_solution(9496104962039874048)
XLA Ops:
  0.6 23.9 %shard_map.194 = (bf16[32,384]{1,0:T(8,128)(2,1)}, f32[12,128]{1,0:T(8,128)}) custom-call(f32[12,32]{1,0:T(8,128)} %refs_0_.1, s32[1,32]{1,0:T(1,128)} %bitcast.16, s32[1,32]{1,0:T(1,128)} %bitcast.17, bf16[32,384]{1,0:T(8,128)(2,1)} %refs_3_.1, bf16[224,192]{1,0:T(8,128)(2,1)} %constant.9.clone.refs_4_, bf16[192,384]{1,0:T(8,128)(2,1)} %bitcast.11, ...), custom_call_target="tpu_custom_call" | custom-call | tf_op jit(solution)/shard_map/pallas_call | solution.py:453
  24.5 0.0 copy-start
  24.6 1.4 %copy.23 = bf16[32,384]{1,0:T(8,128)(2,1)} copy(bf16[32,384]{1,0:T(8,128)(2,1)} %get-tuple-element.4) | data formatting | bytes 49152
  25.9 0.0 copy-done
  25.9 0.6 %copy.24 = f32[12,128]{1,0:T(8,128)} copy(f32[12,128]{1,0:T(8,128)S(1)} %copy-done) | data formatting | bytes 12288
Async XLA Ops:
  24.5 1.4 %copy-start = (f32[12,128]{1,0:T(8,128)S(1)}, f32[12,128]{1,0:T(8,128)}, u32[]{:S(2)}) copy-start(f32[12,128]{1,0:T(8,128)} %get-tuple-element.5) | copy-start | bytes 18436

commit v5 on v4

--- a/solution.py
+++ b/solution.py
@@ -80,7 +80,7 @@
     so_ref, fo_ref = refs[count : count + 2]
     near = dict(zip(ORDER, refs[count + 2 : 2 * count + 2]))
     (
-        gath, meta_s, sp, ex, part, red, so32, fg,
+        gath, meta_s, qb, sp, ex, part, red, so32, fg,
         load_sem, gs_sem, gr_sem, es_sem, er_sem, rs_sem, rr_sem, fs_sem, fr_sem,
         os_sem, or_sem,
     ) = refs[2 * count + 2 :]
@@ -181,6 +181,19 @@
         return out
 
     q_global = moved(q_local, 0, step, frames)
+    for a in range(3):
+        for p in range(queries):
+            for i in range(rows):
+                spot = ((a * queries + p) * rows + i) * SUB
+                qb[spot : spot + SUB, :] = jnp.broadcast_to(
+                    q_global[a][p * SUB : (p + 1) * SUB, i : i + 1], (SUB, LANES)
+                )
+
+    def along_keys(value):
+        if keys <= LANES:
+            return value[:, :keys]
+        return jnp.concatenate([value] * (keys // LANES), axis=1)
+
     eye = (
         lax.broadcasted_iota(jnp.int32, (SUB, heads), 0)
         == lax.broadcasted_iota(jnp.int32, (SUB, heads), 1)
@@ -235,10 +248,8 @@
         distance = jnp.zeros((SUB, keys), f32)
         for a in range(3):
             for p in range(queries):
-                gap = (
-                    q_global[a][p * SUB : (p + 1) * SUB, i : i + 1]
-                    - k_global[a][p * SUB : (p + 1) * SUB, :]
-                )
+                spot = ((a * queries + p) * rows + i) * SUB
+                gap = along_keys(qb[spot : spot + SUB, :]) - k_global[a][p * SUB : (p + 1) * SUB, :]
                 distance = distance + gap * gap
         differ = jnp.where(key_chain != chain_ref[i].astype(f32), chain_term, 0.0)
         logits = LOGIT_WEIGHT * (
@@ -462,6 +473,7 @@
             + [
                 pltpu.VMEM((nb, half, width + LANES), jnp.float32),
                 pltpu.VMEM((rows, LANES), jnp.float32),
+                pltpu.VMEM((3 * queries * rows * SUB, LANES), jnp.float32),
                 pltpu.VMEM((rows * SUB, channels), jnp.float32),
                 pltpu.VMEM((npr, rows, LANES + 3 * wide), jnp.float32),
                 pltpu.VMEM((rows, width), jnp.float32),

time: 26.7 us -> 23.3 us (0.87)
  Pallas kernels: 23.9 us -> 20.5 us
    pallas_call x1, Pallas kernels: 23.9 us -> 20.5 us  [body(): pl.pallas_call(functools.partial(kernel, dims), out_shape=(jax.ShapeDtype...]
where the time goes in v5:
time: 23.3 us; the launch traced here: 23.1 us
  Pallas kernels  20.5 us (88%)
  local copies, waits for them, and re-layouts  1.96 us (8%)
  between operations  0.65 us (3%)
    pallas_call x1, Pallas kernels, body(): pl.pallas_call(functools.partial(kernel, dims), out_shape=(jax.ShapeDtype...  20.5 us
    unnamed x4, local copies, waits for them, and re-layouts  1.96 us

profile of v5, /device:TPU:0, one launch (start us, length us, event | category | flops | bytes accessed | tf_op | source)
XLA Modules:
  0.0 23.1 jit_solution(14800291694374252755)
XLA Ops:
  0.6 20.5 %shard_map.194 = (bf16[32,384]{1,0:T(8,128)(2,1)}, f32[12,128]{1,0:T(8,128)}) custom-call(f32[12,32]{1,0:T(8,128)} %refs_0_.1, s32[1,32]{1,0:T(1,128)} %bitcast.16, s32[1,32]{1,0:T(1,128)} %bitcast.17, bf16[32,384]{1,0:T(8,128)(2,1)} %refs_3_.1, bf16[224,192]{1,0:T(8,128)(2,1)} %constant.9.clone.refs_4_, bf16[192,384]{1,0:T(8,128)(2,1)} %bitcast.11, ...), custom_call_target="tpu_custom_call" | custom-call | tf_op jit(solution)/shard_map/pallas_call | solution.py:464
  21.2 0.0 copy-start
  21.2 1.4 %copy.23 = bf16[32,384]{1,0:T(8,128)(2,1)} copy(bf16[32,384]{1,0:T(8,128)(2,1)} %get-tuple-element.4) | data formatting | bytes 49152
  22.5 0.0 copy-done
  22.5 0.6 %copy.24 = f32[12,128]{1,0:T(8,128)} copy(f32[12,128]{1,0:T(8,128)S(1)} %copy-done) | data formatting | bytes 12288
Async XLA Ops:
  21.2 1.4 %copy-start = (f32[12,128]{1,0:T(8,128)S(1)}, f32[12,128]{1,0:T(8,128)}, u32[]{:S(2)}) copy-start(f32[12,128]{1,0:T(8,128)} %get-tuple-element.5) | copy-start | bytes 18436

commit v6 on v5

--- a/solution.py
+++ b/solution.py
@@ -392,13 +392,13 @@
         turn[9 + a] + sum(turn[3 * a + b] * m[3 + b] for b in range(3)) for a in range(3)
     ]
     lines = jnp.concatenate(lines + [jnp.zeros((4, half), f32)], axis=0)
-    fg[me_b, me_p] = jnp.concatenate([lines, jnp.zeros((16, LANES - half), f32)], axis=1)
+    fg[...] = jnp.concatenate([lines, jnp.zeros((16, LANES - half), f32)], axis=1)
     finals = []
     for d, dp in block:
         code = d * npr + dp
         copy = pltpu.make_async_remote_copy(
-            src_ref=fg.at[me_b, me_p],
-            dst_ref=fg.at[me_b, me_p],
+            src_ref=fg,
+            dst_ref=fo_ref.at[me_b, me_p],
             send_sem=fs_sem.at[code],
             recv_sem=fr_sem.at[code],
             device_id=block_peer(d, dp),
@@ -406,11 +406,11 @@
         )
         copy.start()
         finals.append(copy)
-    so32[me_p] = out.astype(f32)
+    so32[...] = out.astype(f32)
     for d in range(1, npr):
         copy = pltpu.make_async_remote_copy(
-            src_ref=so32.at[me_p],
-            dst_ref=so32.at[me_p],
+            src_ref=so32,
+            dst_ref=so_ref.at[me_p],
             send_sem=os_sem.at[d],
             recv_sem=or_sem.at[d],
             device_id=group_peer(0, d),
@@ -418,16 +418,22 @@
         )
         copy.start()
         finals.append(copy)
-    for copy in finals[len(block) :]:
+    for source, target, slot in ((fg, fo_ref.at[me_b, me_p], fs_sem), (so32, so_ref.at[me_p], os_sem)):
+        copy = pltpu.make_async_copy(source, target, slot.at[0])
+        copy.start()
+        finals.append(copy)
+    for copy in finals:
         copy.wait()
-    for p in range(npr):
-        so_ref[p * half : (p + 1) * half, :] = so32[p].astype(bf16)
-    for copy in finals[: len(block)]:
-        copy.wait()
-    for k in range(nb):
-        for p in range(npr):
-            spot = (k * npr + p) * half
-            fo_ref[:, spot : spot + half] = fg[k, p, :12, :half]
+
+
+def finish(halves_ref, pieces_ref, so_ref, fo_ref):
+    parts, half = halves_ref.shape[:2]
+    for p in range(parts):
+        so_ref[p * half : (p + 1) * half, :] = halves_ref[p].astype(jnp.bfloat16)
+    for k in range(pieces_ref.shape[0]):
+        for p in range(parts):
+            spot = (k * parts + p) * half
+            fo_ref[:, spot : spot + half] = pieces_ref[k, p, :12, :half]
 
 
 def body(
@@ -460,40 +466,50 @@
         (pltpu.SMEM if name in SCALARS else pltpu.VMEM)(given[name].shape, given[name].dtype)
         for name in ORDER
     ]
+    far = pl.BlockSpec(memory_space=pl.ANY)
+    pieces = pl.pallas_call(
+        functools.partial(kernel, dims),
+        out_shape=(
+            jax.ShapeDtypeStruct((npr, half, width), jnp.float32),
+            jax.ShapeDtypeStruct((nb, npr, 16, LANES), jnp.float32),
+        ),
+        in_specs=[far] * len(operands),
+        out_specs=(far, far),
+        scratch_shapes=held
+        + [
+            pltpu.VMEM((nb, half, width + LANES), jnp.float32),
+            pltpu.VMEM((rows, LANES), jnp.float32),
+            pltpu.VMEM((3 * queries * rows * SUB, LANES), jnp.float32),
+            pltpu.VMEM((rows * SUB, channels), jnp.float32),
+            pltpu.VMEM((npr, rows, LANES + 3 * wide), jnp.float32),
+            pltpu.VMEM((rows, width), jnp.float32),
+            pltpu.VMEM((nh * npr, half, width), jnp.float32),
+            pltpu.VMEM((half, width), jnp.float32),
+            pltpu.VMEM((16, LANES), jnp.float32),
+            dma((len(operands),)),
+            dma((nb,)),
+            dma((nb,)),
+            dma((npr,)),
+            dma((npr,)),
+            dma((nh * npr,)),
+            dma((nh * npr,)),
+            dma((nb * npr,)),
+            dma((nb * npr,)),
+            dma((npr,)),
+            dma((npr,)),
+        ],
+        compiler_params=pltpu.CompilerParams(collective_id=0, has_side_effects=True),
+    )(*operands)
     return tuple(
         pl.pallas_call(
-            functools.partial(kernel, dims),
+            finish,
             out_shape=(
                 jax.ShapeDtypeStruct((rows, width), jnp.bfloat16),
                 jax.ShapeDtypeStruct((12, nb * rows), jnp.float32),
             ),
-            in_specs=[pl.BlockSpec(memory_space=pl.ANY)] * len(operands),
+            in_specs=[vmem, vmem],
             out_specs=(vmem, vmem),
-            scratch_shapes=held
-            + [
-                pltpu.VMEM((nb, half, width + LANES), jnp.float32),
-                pltpu.VMEM((rows, LANES), jnp.float32),
-                pltpu.VMEM((3 * queries * rows * SUB, LANES), jnp.float32),
-                pltpu.VMEM((rows * SUB, channels), jnp.float32),
-                pltpu.VMEM((npr, rows, LANES + 3 * wide), jnp.float32),
-                pltpu.VMEM((rows, width), jnp.float32),
-                pltpu.VMEM((nh * npr, half, width), jnp.float32),
-                pltpu.VMEM((npr, half, width), jnp.float32),
-                pltpu.VMEM((nb, npr, 16, LANES), jnp.float32),
-                dma((len(operands),)),
-                dma((nb,)),
-                dma((nb,)),
-                dma((npr,)),
-                dma((npr,)),
-                dma((nh * npr,)),
-                dma((nh * npr,)),
-                dma((nb * npr,)),
-                dma((nb * npr,)),
-                dma((npr,)),
-                dma((npr,)),
-            ],
-            compiler_params=pltpu.CompilerParams(collective_id=0, has_side_effects=True),
-        )(*operands)
+        )(*pieces)
     )
 
 

time: 23.3 us -> 22.6 us (0.970)
  local copies, waits for them, and re-layouts: 1.96 us -> 0 us
  Pallas kernels: 20.5 us -> 21.8 us
    unnamed x4 -> x0, local copies, waits for them, and re-layouts: 1.96 us -> none
    pallas_call x0 -> x1, Pallas kernels: none -> 1.55 us  [body(): pl.pallas_call(finish, out_shape=(jax.ShapeDtypeStruct((rows, width), jnp...]
    pallas_call x1, Pallas kernels: 20.5 us -> 20.2 us  [body(): pl.pallas_call(functools.partial(kernel, dims), out_shape=(jax.ShapeDtype...]
where the time goes in v6:
time: 22.6 us; the launch traced here: 22.4 us
  Pallas kernels  21.8 us (96%)
  between operations  0.64 us (3%)
    pallas_call x1, Pallas kernels, body(): pl.pallas_call(functools.partial(kernel, dims), out_shape=(jax.ShapeDtype...  20.2 us
    pallas_call x1, Pallas kernels, body(): pl.pallas_call(finish, out_shape=(jax.ShapeDtypeStruct((rows, width), jnp...  1.55 us

profile of v6, /device:TPU:0, one launch (start us, length us, event | category | flops | bytes accessed | tf_op | source)
XLA Modules:
  0.0 22.4 jit_solution(4858189774612506751)
XLA Ops:
  0.6 20.2 %shard_map.194 = (f32[2,16,384]{2,1,0:T(8,128)}, f32[4,2,16,128]{3,2,1,0:T(8,128)}) custom-call(f32[12,32]{1,0:T(8,128)} %refs_0_.1, s32[1,32]{1,0:T(1,128)} %bitcast.16, s32[1,32]{1,0:T(1,128)} %bitcast.17, bf16[32,384]{1,0:T(8,128)(2,1)} %refs_3_.1, bf16[224,192]{1,0:T(8,128)(2,1)} %constant.9.clone.refs_4_, bf16[192,384]{1,0:T(8,128)(2,1)} %bitcast.11, ...), custom_call_target="tpu_custom_call" | custom-call | tf_op jit(solution)/shard_map/pallas_call | solution.py:470
  20.9 1.6 %shard_map.195 = (bf16[32,384]{1,0:T(8,128)(2,1)}, f32[12,128]{1,0:T(8,128)}) custom-call(f32[2,16,384]{2,1,0:T(8,128)} %get-tuple-element.4.halves_ref, f32[4,2,16,128]{3,2,1,0:T(8,128)} %get-tuple-element.5.pieces_ref), custom_call_target="tpu_custom_call" | custom-call | tf_op jit(solution)/shard_map/pallas_call | solution.py:504

commit v7 on v6

--- a/solution.py
+++ b/solution.py
@@ -332,28 +332,34 @@
     ]
     norms = jnp.sqrt(sum(p * p for p in pointed) + 1.0)
     features = [attended] + [p * (1.0 / npr) for p in pointed + [norms]]
-    partial = sum(
-        nn(feature.astype(bf16), w_small[k * wide : (k + 1) * wide])
-        for k, feature in enumerate(features)
-    )
-    for h in range(heads):
-        paired = sp[pl.ds(h, rows, stride=SUB), :] * factors[0][:, h : h + 1]
-        partial = partial + nn(paired.astype(bf16), wout_v[h, small:, :])
-    part[...] = partial
+    features = [feature.astype(bf16) for feature in features]
+    paired = [
+        (sp[pl.ds(h, rows, stride=SUB), :] * factors[0][:, h : h + 1]).astype(bf16)
+        for h in range(heads)
+    ]
+    cuts = [slice(k, min(k + 2 * LANES, width)) for k in range(0, width, 2 * LANES)]
     reductions = []
-    for dh, dp in group:
-        code = dh * npr + dp
-        target = pl.multiple_of(lax.rem(me_p + dp, npr) * half, half)
-        copy = pltpu.make_async_remote_copy(
-            src_ref=part.at[pl.ds(target, half)],
-            dst_ref=red.at[code],
-            send_sem=rs_sem.at[code],
-            recv_sem=rr_sem.at[code],
-            device_id=group_peer(dh, dp),
-            device_id_type=MESH,
-        )
-        copy.start()
-        reductions.append(copy)
+    for number, columns in enumerate(cuts):
+        partial = sum(
+            nn(feature, w_small[k * wide : (k + 1) * wide, columns])
+            for k, feature in enumerate(features)
+        )
+        for h in range(heads):
+            partial = partial + nn(paired[h], wout_v[h, small:, columns])
+        part[:, columns] = partial
+        for dh, dp in reversed(group):
+            code = dh * npr + dp
+            target = pl.multiple_of(lax.rem(me_p + dp, npr) * half, half)
+            copy = pltpu.make_async_remote_copy(
+                src_ref=part.at[pl.ds(target, half), columns],
+                dst_ref=red.at[code, :, columns],
+                send_sem=rs_sem.at[number, code],
+                recv_sem=rr_sem.at[number, code],
+                device_id=group_peer(dh, dp),
+                device_id_type=MESH,
+            )
+            copy.start()
+            reductions.append(copy)
     red[0] = part[pl.ds(start, half), :]
     for copy, landing in gathers:
         copy.wait_send()
@@ -491,8 +497,8 @@
             dma((nb,)),
             dma((npr,)),
             dma((npr,)),
-            dma((nh * npr,)),
-            dma((nh * npr,)),
+            dma((-(-width // (2 * LANES)), nh * npr)),
+            dma((-(-width // (2 * LANES)), nh * npr)),
             dma((nb * npr,)),
             dma((nb * npr,)),
             dma((npr,)),

time: 22.6 us -> 22.7 us (level)
  no operation moved by 1% of the time
where the time goes in v7:
time: 22.7 us; the launch traced here: 22.5 us
  Pallas kernels  21.9 us (96%)
  between operations  0.64 us (3%)
    pallas_call x1, Pallas kernels, body(): pl.pallas_call(functools.partial(kernel, dims), out_shape=(jax.ShapeDtype...  20.3 us
    pallas_call x1, Pallas kernels, body(): pl.pallas_call(finish, out_shape=(jax.ShapeDtypeStruct((rows, width), jnp...  1.55 us

profile of v7, /device:TPU:0, one launch (start us, length us, event | category | flops | bytes accessed | tf_op | source)
XLA Modules:
  0.0 22.5 jit_solution(13331952178735722098)
XLA Ops:
  0.6 20.3 %shard_map.194 = (f32[2,16,384]{2,1,0:T(8,128)}, f32[4,2,16,128]{3,2,1,0:T(8,128)}) custom-call(f32[12,32]{1,0:T(8,128)} %refs_0_.1, s32[1,32]{1,0:T(1,128)} %bitcast.16, s32[1,32]{1,0:T(1,128)} %bitcast.17, bf16[32,384]{1,0:T(8,128)(2,1)} %refs_3_.1, bf16[224,192]{1,0:T(8,128)(2,1)} %constant.9.clone.refs_4_, bf16[192,384]{1,0:T(8,128)(2,1)} %bitcast.11, ...), custom_call_target="tpu_custom_call" | custom-call | tf_op jit(solution)/shard_map/pallas_call | solution.py:476
  21.0 1.6 %shard_map.195 = (bf16[32,384]{1,0:T(8,128)(2,1)}, f32[12,128]{1,0:T(8,128)}) custom-call(f32[2,16,384]{2,1,0:T(8,128)} %get-tuple-element.4.halves_ref, f32[4,2,16,128]{3,2,1,0:T(8,128)} %get-tuple-element.5.pieces_ref), custom_call_target="tpu_custom_call" | custom-call | tf_op jit(solution)/shard_map/pallas_call | solution.py:510
